TPU v7x, 512 devices: a whole 4x4x16 slice. The times are simulated.
512 devices in a mesh: cfg: 2 (over y_hi), seq: 32 (over z, core), tp: 8 (over x, y_lo).
Axes of the slice: x: 4, y: 4 (y_hi: 2, y_lo: 2; y = y_hi * 2 + y_lo), z: 16, core: 2. Of those that a mesh axis runs over, the one named last changes fastest.
Arguments:
- stream: bfloat16 [2, 12288, 3072], P('cfg', 'seq', 'tp'), may hold values from -1.5 to 1.5
- qkv: bfloat16 [2, 12288, 3, 3072], P('cfg', 'seq', None, 'tp'), may hold values from -400 to 400
- q_gain: float32 [128], replicated, may hold values from 0.5 to 6
- k_gain: float32 [128], replicated, may hold values from 0.5 to 6
- w_out: bfloat16 [3072, 3072], P('tp'), may hold values from -0.109375 to 0.109375
- mod: float32 [2, 8, 3, 3072], P('cfg'), may hold values from -4 to 4
- w_proj: bfloat16 [64, 3072], replicated, may hold values from -0.109375 to 0.109375
- latent: float32 [6144, 128], P('seq'), may hold values from -6 to 6
- guidance: float32 [8], replicated, may hold values from 2 to 6
- img_counts: int32 [8], replicated, may hold values from 1 to 2816, 11264 in all
- img_widths: int32 [8], replicated, may hold values from 16 to 64
- step_index: int32 [8], replicated, may hold values from 0 to 7
Outputs:
- velocity: float32 [6144, 128], P('seq', 'cfg')
- next_latent: float32 [6144, 128], P('seq', 'cfg')
- top_logit: float32 [2, 24], P('cfg', 'tp')
Inputs may be any that keep to these rules, and one draw needn't show every extreme that they name: Request r holds 128 text rows followed by img_counts[r] image rows; requests lie end to end in order and fill all 12288 rows; the counts sum to 11264 and the largest is exactly 2816.
All inputs are finite; a program needn't handle non-finite values.
Results may differ from a plain program's by a relative error of at most 0.017.
The roundings to bfloat16 on the way count: a program that leaves them out, or rounds other values in their place, can miss the bound.
Values may be sent and summed in bfloat16 or wider, within the bound.
A program may use at most 64 MiB of HBM per device.

v0:
```python
import math

import jax
import jax.numpy as jnp
import numpy as np
from jax import lax
from jax.sharding import PartitionSpec as P

HDIM = 128
CH = 64
TXT = 128
STEPS = 8


PHI_MIX = 0.7
NEG_FLOOR = -1e30


def from_behind(block, axis, distance):
    devices = range(lax.axis_size(axis))
    route = [(i - distance, i) for i in devices if i - distance in devices]
    return lax.ppermute(block, axis, route)


def swapped(value, axis, stride):
    mask = 2**stride
    pairs = [(source, source ^ mask) for source in range(lax.axis_size(axis))]
    return lax.ppermute(value, axis, pairs)


def rope_tables():
    pair_index = np.arange(64)
    axis_of = np.where(pair_index < 8, 0, np.where(pair_index < 36, 1, 2))
    axis_start = np.array([0, 8, 36])[axis_of]
    axis_width = np.array([16.0, 56.0, 56.0])[axis_of]
    frequency = 10000.0 ** (-2.0 * (pair_index - axis_start) / axis_width)
    return (np.repeat(axis_of, 2), np.repeat(frequency, 2))


def row_layout(first_row, row_count, img_counts):
    lengths = TXT + img_counts
    row_ends = jnp.cumsum(lengths)
    starts = row_ends - lengths
    row_ids = first_row + jnp.arange(row_count, dtype=jnp.int32)
    request = jnp.sum((row_ids[:, None] >= row_ends[None, :]).astype(jnp.int32), axis=1)
    request_hot = request[:, None] == jnp.arange(img_counts.shape[0], dtype=jnp.int32)[None, :]
    start_row = jnp.sum(jnp.where(request_hot, starts[None, :], 0), axis=1)
    local_row = row_ids - start_row
    is_image = local_row >= TXT
    image_pos = jnp.maximum(local_row - TXT, 0)
    return (request, request_hot, is_image, image_pos)


def rope_angles(is_image, image_pos, request_hot, img_widths):
    axis_of, frequency = rope_tables()
    width_row = jnp.sum(jnp.where(request_hot, img_widths[None, :], 0), axis=1)
    width_row = jnp.maximum(width_row, 1)
    id_height = jnp.where(is_image, image_pos // width_row, 0)
    id_width = jnp.where(is_image, image_pos % width_row, 0)
    on_height = jnp.asarray(axis_of == 1)[None, :]
    on_width = jnp.asarray(axis_of == 2)[None, :]
    position = jnp.where(on_height, id_height[:, None], jnp.where(on_width, id_width[:, None], 0))
    angles = position.astype(jnp.float32) * jnp.asarray(frequency, jnp.float32)[None, :]
    return (jnp.cos(angles)[:, None, :], jnp.sin(angles)[:, None, :])


def head_norm(values, gain):
    mean_square = jnp.mean(values * values, axis=-1, keepdims=True)
    return values * lax.rsqrt(mean_square + 1e-06) * gain


def rotary(values, angle_cos, angle_sin):
    channel = jnp.arange(values.shape[-1], dtype=jnp.int32)
    is_even = channel % 2 == 0
    partner = jnp.where(is_even, -jnp.roll(values, -1, axis=-1), jnp.roll(values, 1, axis=-1))
    return values * angle_cos + partner * angle_sin


def pick_rows(hot_float, table):
    return jnp.dot(
        hot_float, table, precision=lax.Precision.HIGHEST, preferred_element_type=jnp.float32
    )


def spread_rows(token_values, row_count):
    return jnp.broadcast_to(token_values[:, None], (row_count, CH)).reshape(row_count // 2, 2 * CH)


def sigma_at(step_value):
    remaining = 1.0 - step_value / STEPS
    return 3.0 * remaining / (1.0 + 2.0 * remaining)


def local(
    stream,
    qkv,
    q_gain,
    k_gain,
    w_out,
    mod,
    w_proj,
    latent,
    guidance,
    img_counts,
    img_widths,
    step_index,
):
    tok_rows = stream.shape[1]
    local_width = qkv.shape[3]
    heads_local = local_width // HDIM
    seq_count = lax.axis_size("seq")
    seq_index = lax.axis_index("seq")
    total_rows = tok_rows * seq_count
    request, request_hot, is_image, image_pos = row_layout(
        seq_index * tok_rows, tok_rows, img_counts
    )
    angle_cos, angle_sin = rope_angles(is_image, image_pos, request_hot, img_widths)
    hot_float = request_hot.astype(jnp.float32)
    scale_root = math.sqrt(float(HDIM))
    query = head_norm(qkv[0, :, 0].astype(jnp.float32).reshape(tok_rows, heads_local, HDIM), q_gain)
    query = rotary(query, angle_cos, angle_sin).astype(jnp.bfloat16)
    key_rows = head_norm(
        qkv[0, :, 1].astype(jnp.float32).reshape(tok_rows, heads_local, HDIM), k_gain
    )
    key_rows = rotary(key_rows, angle_cos, angle_sin).astype(jnp.bfloat16)
    value_rows = qkv[0, :, 2].reshape(tok_rows, heads_local, HDIM)

    def attend(attn_state, key_block, value_block, source):
        key_request = row_layout(source * tok_rows, tok_rows, img_counts)[0]
        in_range = (source >= 0) & (source < seq_count)
        touches = in_range & (request[-1] >= key_request[0]) & (key_request[-1] >= request[0])

        def update(carried):
            running_max, running_sum, running_acc, running_top = carried
            scores = (
                jnp.einsum("qhd,khd->hqk", query, key_block, preferred_element_type=jnp.float32)
                / scale_root
            )
            same_request = request[:, None] == key_request[None, :]
            scores = jnp.where(same_request[None], scores, -jnp.inf)
            new_max = jnp.maximum(running_max, jnp.max(scores, axis=-1))
            weights = jnp.exp(scores - new_max[..., None])
            shrink = jnp.exp(running_max - new_max)
            new_sum = running_sum * shrink + jnp.sum(weights, axis=-1)
            new_acc = running_acc * shrink.T[:, :, None] + jnp.einsum(
                "hqk,khd->qhd",
                weights.astype(jnp.bfloat16),
                value_block,
                preferred_element_type=jnp.float32,
            )
            new_top = jnp.maximum(running_top, jnp.max(scores, axis=(1, 2)))
            return (new_max, new_sum, new_acc, new_top)

        return lax.cond(touches, update, lambda carried: carried, attn_state)

    attn_state = (
        jnp.full((heads_local, tok_rows), NEG_FLOOR, jnp.float32),
        jnp.zeros((heads_local, tok_rows), jnp.float32),
        jnp.zeros((tok_rows, heads_local, HDIM), jnp.float32),
        jnp.full((heads_local,), NEG_FLOOR, jnp.float32),
    )
    img_most = (total_rows - img_counts.shape[0] * TXT) // 4
    reach_blocks = (TXT + img_most + tok_rows - 2) // tok_rows
    attn_state = attend(attn_state, key_rows, value_rows, seq_index)

    def window_turn(turn_index, loop_carry):
        window_state, fwd_key, fwd_value, back_key, back_value = loop_carry
        fwd_key, fwd_value = from_behind((fwd_key, fwd_value), "seq", 1)
        window_state = attend(window_state, fwd_key, fwd_value, seq_index - turn_index - 1)
        back_key, back_value = from_behind((back_key, back_value), "seq", -1)
        window_state = attend(window_state, back_key, back_value, seq_index + turn_index + 1)
        return (window_state, fwd_key, fwd_value, back_key, back_value)

    attn_state = lax.fori_loop(
        0, reach_blocks, window_turn, (attn_state, key_rows, value_rows, key_rows, value_rows)
    )[0]
    final_max, final_sum, final_acc, final_top = attn_state
    attended = (
        (final_acc / final_sum.T[:, :, None]).astype(jnp.bfloat16).reshape(tok_rows, local_width)
    )
    top_scores = lax.pmax(final_top, "seq")
    partial_out = jnp.dot(attended, w_out, preferred_element_type=jnp.float32)
    projected = lax.psum(partial_out.astype(jnp.bfloat16), "tp").astype(jnp.float32)
    residual = lax.all_gather(stream[0], "tp", axis=1, tiled=True).astype(jnp.float32)
    gate = pick_rows(hot_float, mod[0, :, 0])
    scale_row = pick_rows(hot_float, mod[0, :, 1])
    shift_row = pick_rows(hot_float, mod[0, :, 2])
    mixed = residual + gate * projected
    centred = mixed - jnp.mean(mixed, axis=1, keepdims=True)
    variance = jnp.mean(centred * centred, axis=1, keepdims=True)
    normed = (centred * lax.rsqrt(variance + 1e-06) * (1.0 + scale_row) + shift_row).astype(
        jnp.bfloat16
    )
    velocity_own = jnp.dot(normed, w_proj.T, preferred_element_type=jnp.float32).reshape(
        tok_rows // 2, 2 * CH
    )
    velocity_other = swapped(velocity_own.astype(jnp.bfloat16), "cfg", 0).astype(velocity_own.dtype)
    cfg_index = lax.axis_index("cfg")
    first_group = cfg_index == 0
    cond_vel = jnp.where(first_group, velocity_own, velocity_other)
    uncond_vel = jnp.where(first_group, velocity_other, velocity_own)
    guide_row = jnp.sum(hot_float * guidance[None, :], axis=1)
    guided = uncond_vel + spread_rows(guide_row, tok_rows) * (cond_vel - uncond_vel)
    image_mask = is_image.astype(jnp.float32)
    cond_square = jnp.sum((cond_vel * cond_vel).reshape(tok_rows, CH), axis=1) * image_mask
    guided_square = jnp.sum((guided * guided).reshape(tok_rows, CH), axis=1) * image_mask
    cond_total, guided_total = lax.psum(
        (
            jnp.sum(hot_float * cond_square[:, None], axis=0),
            jnp.sum(hot_float * guided_square[:, None], axis=0),
        ),
        "seq",
    )
    entries = img_counts.astype(jnp.float32) * CH
    factor = (PHI_MIX * jnp.sqrt(cond_total / entries + 1e-06) + (1.0 - PHI_MIX)) / jnp.sqrt(
        guided_total / entries + 1e-06
    )
    factor_row = jnp.sum(hot_float * factor[None, :], axis=1) * image_mask
    velocity = guided * spread_rows(factor_row, tok_rows)
    step_float = step_index.astype(jnp.float32)
    delta = sigma_at(step_float + 1.0) - sigma_at(step_float)
    delta_row = jnp.sum(hot_float * delta[None, :], axis=1)
    next_latent = latent + spread_rows(delta_row, tok_rows) * velocity
    col_first = cfg_index * CH
    velocity_half = lax.dynamic_slice_in_dim(velocity, col_first, CH, 1)
    latent_half = lax.dynamic_slice_in_dim(next_latent, col_first, CH, 1)
    return (velocity_half, latent_half, top_scores.reshape(1, heads_local))


def solution(mesh):
    placed = (
        P("cfg", "seq", "tp"),
        P("cfg", "seq", None, "tp"),
        P(),
        P(),
        P("tp", None),
        P("cfg", None, None, None),
        P(),
        P("seq", None),
        P(),
        P(),
        P(),
        P(),
    )
    return jax.shard_map(
        local,
        mesh=mesh,
        in_specs=placed,
        out_specs=(P("seq", "cfg"), P("seq", "cfg"), P("cfg", "tp")),
        check_vma=False,
    )
```

profile of v0, /device:TPU:1, one launch (start us, length us, event | category | flops | bytes accessed | tf_op | source)
XLA Modules:
  0.0 619.1 jit_solution(9478542159529023892)
XLA Ops:
  25.9 4.3 conditional.3
  30.8 260.4 %while.29 = (s32[]{:T(128)}, f32[3,384]{1,0:T(4,128)}, f32[3,384]{1,0:T(4,128)S(1)}, f32[384,3,128]{2,0,1:T(8,128)S(1)}, f32[3]{0:T(128)}, /*index=5*/bf16[384,3...) while((s32[]{:T(128)}, f32[3,384]{1,0:T(4,128)}, ...), condition=%wide.region_25.26_spmd, body=%wide.region_11.25_spmd.sunk | while | flops 460972864 | bytes 22583836 | solution.py:174
  30.8 4.9 collective-permute-start
  37.6 5.2 collective-permute-start.2
  54.8 5.4 conditional.6
  60.2 5.7 conditional.7
  91.7 5.7 conditional.7
  103.2 9.0 %collective-permute-start = (bf16[384,3,128]{2,0,1:T(8,128)(2,1)}, bf16[384,3,128]{2,0,1:T(8,128)(2,1)}, u32[]{:S(2)}, u32[]{:S(2)}) collective-permute-start(bf16[384,3,128]{2,0,1:T(8,128)(2,1)} %get-tuple-element.744), channel_id=1, source_target_pairs={{0,8},{8,16},{16,24},{24,32},{32,40},{40,48},{48,56},{56,64},{64,7... | collective-permute-start | bytes 884744 | tf_op jit(solution)/shard_map/while/body/eval_jaxpr/ppermute | solution.py:22
  128.6 5.7 conditional.7
  140.1 3.6 collective-permute-start
  143.7 7.3 %collective-permute-start.1 = (bf16[384,3,128]{2,0,1:T(8,128)(2,1)}, bf16[384,3,128]{2,0,1:T(8,128)(2,1)S(1)}, u32[]{:S(2)}, u32[]{:S(2)}) collective-permute-start(bf16[384,3,128]{2,0,1:T(8,128)(2,1)} %get-tuple-element.745), channel_id=1, source_target_pairs={{0,8},{8,16},{16,24},{24,32},{32,40},{40,48},{48,56},{56,64},{64,7... | collective-permute-start | bytes 884744 | tf_op jit(solution)/shard_map/while/body/eval_jaxpr/ppermute | solution.py:22
  165.0 5.7 conditional.7
  196.5 5.7 conditional.7
  208.0 3.6 collective-permute-start
  228.0 5.7 conditional.7
  263.7 3.6 collective-permute-start
  269.3 4.1 collective-permute-start.2
  297.2 4.2 fusion.34
  301.3 129.8 %all-reduce.3.cloned.1.call-done = bf16[384,3072]{1,0:T(8,128)(2,1)} async-done(((bf16[384,3072]{1,0:T(8,128)(2,1)}), bf16[384,3072]{1,0:T(8,128)(2,1)}) %all-reduce.3.cloned.1.call-update) | async-done | bytes 2359312 | tf_op jit(solution)/shard_map/psum | solution.py:183
  431.1 64.9 %all-gather.3.cloned.1.call-done = bf16[1,384,3072]{2,1,0:T(8,128)(2,1)} async-done(((bf16[1,384,384]{2,1,0:T(8,128)(2,1)}), bf16[1,384,3072]{2,1,0:T(8,128)(2,1)}) %all-gather.3.cloned.1.call-update) | async-done | bytes 2359312 | tf_op jit(solution)/shard_map/all_gather | solution.py:184
  496.0 5.0 fusion.67
  507.0 5.9 collective-permute-start.4
  513.0 48.5 %pmax.7 = f32[1,3]{1,0:T(1,128)} all-reduce(f32[1,3]{1,0:T(1,128)S(1)} %bitcast.95), channel_id=1, replica_groups=mesh['cfg'=2,'seq'=32,'tp'=8] {'seq'}, use_global_device_ids=true, to_apply=%region_38.39 | all-reduce | flops 3 | bytes 24 | tf_op jit(solution)/shard_map/pmax | solution.py:181
  562.7 47.1 %all-reduce = (f32[8]{0:T(128)S(1)}, f32[8]{0:T(128)S(1)}) all-reduce(f32[8]{0:T(128)S(1)} %get-tuple-element.506, f32[8]{0:T(128)S(1)} %get-tuple-element.505), channel_id=1, replica_groups=mesh['cfg'=2,'seq'=32,'tp'=8] {'seq'}, use_global_device_ids=true, to_apply=%region_35.36 | all-reduce | flops 16 | bytes 128 | tf_op jit(solution)/shard_map/psum | solution.py:207
  (394 shorter events, 216.0 us)
Async XLA Ops:
  7.2 423.9 %all-reduce.3.cloned.1.call-start = ((), (), s32[]{:S(2)}) async-start(), calls=%async_computation | async-start | bytes 4718592 | tf_op jit(solution)/shard_map/psum | solution.py:183
  30.8 24.0 %collective-permute-start = (bf16[384,3,128]{2,0,1:T(8,128)(2,1)}, bf16[384,3,128]{2,0,1:T(8,128)(2,1)}, u32[]{:S(2)}, u32[]{:S(2)}) collective-permute-start(bf16[384,3,128]{2,0,1:T(8,128)(2,1)} %get-tuple-element.744), channel_id=1, source_target_pairs={{0,8},{8,16},{16,24},{24,32},{32,40},{40,48},{48,56},{56,64},{64,7... | collective-permute-start | bytes 884744 | tf_op jit(solution)/shard_map/while/body/eval_jaxpr/ppermute | solution.py:22
  35.7 19.1 %collective-permute-start.1 = (bf16[384,3,128]{2,0,1:T(8,128)(2,1)}, bf16[384,3,128]{2,0,1:T(8,128)(2,1)S(1)}, u32[]{:S(2)}, u32[]{:S(2)}) collective-permute-start(bf16[384,3,128]{2,0,1:T(8,128)(2,1)} %get-tuple-element.745), channel_id=1, source_target_pairs={{0,8},{8,16},{16,24},{24,32},{32,40},{40,48},{48,56},{56,64},{64,7... | collective-permute-start | bytes 884744 | tf_op jit(solution)/shard_map/while/body/eval_jaxpr/ppermute | solution.py:22
  37.6 22.6 %collective-permute-start.2 = (bf16[384,3,128]{2,0,1:T(8,128)(2,1)}, bf16[384,3,128]{2,0,1:T(8,128)(2,1)}, u32[]{:S(2)}, u32[]{:S(2)}) collective-permute-start(bf16[384,3,128]{2,0,1:T(8,128)(2,1)} %get-tuple-element.746), channel_id=1, source_target_pairs={{8,0},{16,8},{24,16},{32,24},{40,32},{48,40},{56,48},{64,56},{72,6... | collective-permute-start | bytes 884744 | tf_op jit(solution)/shard_map/while/body/eval_jaxpr/ppermute | solution.py:22
  42.8 17.4 %collective-permute-start.3 = (bf16[384,3,128]{2,0,1:T(8,128)(2,1)}, bf16[384,3,128]{2,0,1:T(8,128)(2,1)}, u32[]{:S(2)}, u32[]{:S(2)}) collective-permute-start(bf16[384,3,128]{2,0,1:T(8,128)(2,1)} %get-tuple-element.747), channel_id=1, source_target_pairs={{8,0},{16,8},{24,16},{32,24},{40,32},{48,40},{56,48},{64,56},{72,6... | collective-permute-start | bytes 884744 | tf_op jit(solution)/shard_map/while/body/eval_jaxpr/ppermute | solution.py:22
  71.7 19.9 %collective-permute-start = (bf16[384,3,128]{2,0,1:T(8,128)(2,1)}, bf16[384,3,128]{2,0,1:T(8,128)(2,1)}, u32[]{:S(2)}, u32[]{:S(2)}) collective-permute-start(bf16[384,3,128]{2,0,1:T(8,128)(2,1)} %get-tuple-element.744), channel_id=1, source_target_pairs={{0,8},{8,16},{16,24},{24,32},{32,40},{40,48},{48,56},{56,64},{64,7... | collective-permute-start | bytes 884744 | tf_op jit(solution)/shard_map/while/body/eval_jaxpr/ppermute | solution.py:22
  75.3 16.3 %collective-permute-start.1 = (bf16[384,3,128]{2,0,1:T(8,128)(2,1)}, bf16[384,3,128]{2,0,1:T(8,128)(2,1)S(1)}, u32[]{:S(2)}, u32[]{:S(2)}) collective-permute-start(bf16[384,3,128]{2,0,1:T(8,128)(2,1)} %get-tuple-element.745), channel_id=1, source_target_pairs={{0,8},{8,16},{16,24},{24,32},{32,40},{40,48},{48,56},{56,64},{64,7... | collective-permute-start | bytes 884744 | tf_op jit(solution)/shard_map/while/body/eval_jaxpr/ppermute | solution.py:22
  77.3 14.4 %collective-permute-start.2 = (bf16[384,3,128]{2,0,1:T(8,128)(2,1)}, bf16[384,3,128]{2,0,1:T(8,128)(2,1)}, u32[]{:S(2)}, u32[]{:S(2)}) collective-permute-start(bf16[384,3,128]{2,0,1:T(8,128)(2,1)} %get-tuple-element.746), channel_id=1, source_target_pairs={{8,0},{16,8},{24,16},{32,24},{40,32},{48,40},{56,48},{64,56},{72,6... | collective-permute-start | bytes 884744 | tf_op jit(solution)/shard_map/while/body/eval_jaxpr/ppermute | solution.py:22
  103.2 25.3 %collective-permute-start = (bf16[384,3,128]{2,0,1:T(8,128)(2,1)}, bf16[384,3,128]{2,0,1:T(8,128)(2,1)}, u32[]{:S(2)}, u32[]{:S(2)}) collective-permute-start(bf16[384,3,128]{2,0,1:T(8,128)(2,1)} %get-tuple-element.744), channel_id=1, source_target_pairs={{0,8},{8,16},{16,24},{24,32},{32,40},{40,48},{48,56},{56,64},{64,7... | collective-permute-start | bytes 884744 | tf_op jit(solution)/shard_map/while/body/eval_jaxpr/ppermute | solution.py:22
  112.2 16.3 %collective-permute-start.1 = (bf16[384,3,128]{2,0,1:T(8,128)(2,1)}, bf16[384,3,128]{2,0,1:T(8,128)(2,1)S(1)}, u32[]{:S(2)}, u32[]{:S(2)}) collective-permute-start(bf16[384,3,128]{2,0,1:T(8,128)(2,1)} %get-tuple-element.745), channel_id=1, source_target_pairs={{0,8},{8,16},{16,24},{24,32},{32,40},{40,48},{48,56},{56,64},{64,7... | collective-permute-start | bytes 884744 | tf_op jit(solution)/shard_map/while/body/eval_jaxpr/ppermute | solution.py:22
  140.1 24.8 %collective-permute-start = (bf16[384,3,128]{2,0,1:T(8,128)(2,1)}, bf16[384,3,128]{2,0,1:T(8,128)(2,1)}, u32[]{:S(2)}, u32[]{:S(2)}) collective-permute-start(bf16[384,3,128]{2,0,1:T(8,128)(2,1)} %get-tuple-element.744), channel_id=1, source_target_pairs={{0,8},{8,16},{16,24},{24,32},{32,40},{40,48},{48,56},{56,64},{64,7... | collective-permute-start | bytes 884744 | tf_op jit(solution)/shard_map/while/body/eval_jaxpr/ppermute | solution.py:22
  143.7 21.2 %collective-permute-start.1 = (bf16[384,3,128]{2,0,1:T(8,128)(2,1)}, bf16[384,3,128]{2,0,1:T(8,128)(2,1)S(1)}, u32[]{:S(2)}, u32[]{:S(2)}) collective-permute-start(bf16[384,3,128]{2,0,1:T(8,128)(2,1)} %get-tuple-element.745), channel_id=1, source_target_pairs={{0,8},{8,16},{16,24},{24,32},{32,40},{40,48},{48,56},{56,64},{64,7... | collective-permute-start | bytes 884744 | tf_op jit(solution)/shard_map/while/body/eval_jaxpr/ppermute | solution.py:22
  176.5 19.9 %collective-permute-start = (bf16[384,3,128]{2,0,1:T(8,128)(2,1)}, bf16[384,3,128]{2,0,1:T(8,128)(2,1)}, u32[]{:S(2)}, u32[]{:S(2)}) collective-permute-start(bf16[384,3,128]{2,0,1:T(8,128)(2,1)} %get-tuple-element.744), channel_id=1, source_target_pairs={{0,8},{8,16},{16,24},{24,32},{32,40},{40,48},{48,56},{56,64},{64,7... | collective-permute-start | bytes 884744 | tf_op jit(solution)/shard_map/while/body/eval_jaxpr/ppermute | solution.py:22
  180.1 16.3 %collective-permute-start.1 = (bf16[384,3,128]{2,0,1:T(8,128)(2,1)}, bf16[384,3,128]{2,0,1:T(8,128)(2,1)S(1)}, u32[]{:S(2)}, u32[]{:S(2)}) collective-permute-start(bf16[384,3,128]{2,0,1:T(8,128)(2,1)} %get-tuple-element.745), channel_id=1, source_target_pairs={{0,8},{8,16},{16,24},{24,32},{32,40},{40,48},{48,56},{56,64},{64,7... | collective-permute-start | bytes 884744 | tf_op jit(solution)/shard_map/while/body/eval_jaxpr/ppermute | solution.py:22
  208.0 20.0 %collective-permute-start = (bf16[384,3,128]{2,0,1:T(8,128)(2,1)}, bf16[384,3,128]{2,0,1:T(8,128)(2,1)}, u32[]{:S(2)}, u32[]{:S(2)}) collective-permute-start(bf16[384,3,128]{2,0,1:T(8,128)(2,1)} %get-tuple-element.744), channel_id=1, source_target_pairs={{0,8},{8,16},{16,24},{24,32},{32,40},{40,48},{48,56},{56,64},{64,7... | collective-permute-start | bytes 884744 | tf_op jit(solution)/shard_map/while/body/eval_jaxpr/ppermute | solution.py:22
  211.6 16.3 %collective-permute-start.1 = (bf16[384,3,128]{2,0,1:T(8,128)(2,1)}, bf16[384,3,128]{2,0,1:T(8,128)(2,1)S(1)}, u32[]{:S(2)}, u32[]{:S(2)}) collective-permute-start(bf16[384,3,128]{2,0,1:T(8,128)(2,1)} %get-tuple-element.745), channel_id=1, source_target_pairs={{0,8},{8,16},{16,24},{24,32},{32,40},{40,48},{48,56},{56,64},{64,7... | collective-permute-start | bytes 884744 | tf_op jit(solution)/shard_map/while/body/eval_jaxpr/ppermute | solution.py:22
  239.5 18.3 %collective-permute-start = (bf16[384,3,128]{2,0,1:T(8,128)(2,1)}, bf16[384,3,128]{2,0,1:T(8,128)(2,1)}, u32[]{:S(2)}, u32[]{:S(2)}) collective-permute-start(bf16[384,3,128]{2,0,1:T(8,128)(2,1)} %get-tuple-element.744), channel_id=1, source_target_pairs={{0,8},{8,16},{16,24},{24,32},{32,40},{40,48},{48,56},{56,64},{64,7... | collective-permute-start | bytes 884744 | tf_op jit(solution)/shard_map/while/body/eval_jaxpr/ppermute | solution.py:22
  241.4 16.4 %collective-permute-start.1 = (bf16[384,3,128]{2,0,1:T(8,128)(2,1)}, bf16[384,3,128]{2,0,1:T(8,128)(2,1)S(1)}, u32[]{:S(2)}, u32[]{:S(2)}) collective-permute-start(bf16[384,3,128]{2,0,1:T(8,128)(2,1)} %get-tuple-element.745), channel_id=1, source_target_pairs={{0,8},{8,16},{16,24},{24,32},{32,40},{40,48},{48,56},{56,64},{64,7... | collective-permute-start | bytes 884744 | tf_op jit(solution)/shard_map/while/body/eval_jaxpr/ppermute | solution.py:22
  243.4 14.5 %collective-permute-start.2 = (bf16[384,3,128]{2,0,1:T(8,128)(2,1)}, bf16[384,3,128]{2,0,1:T(8,128)(2,1)}, u32[]{:S(2)}, u32[]{:S(2)}) collective-permute-start(bf16[384,3,128]{2,0,1:T(8,128)(2,1)} %get-tuple-element.746), channel_id=1, source_target_pairs={{8,0},{16,8},{24,16},{32,24},{40,32},{48,40},{56,48},{64,56},{72,6... | collective-permute-start | bytes 884744 | tf_op jit(solution)/shard_map/while/body/eval_jaxpr/ppermute | solution.py:22
  263.7 21.6 %collective-permute-start = (bf16[384,3,128]{2,0,1:T(8,128)(2,1)}, bf16[384,3,128]{2,0,1:T(8,128)(2,1)}, u32[]{:S(2)}, u32[]{:S(2)}) collective-permute-start(bf16[384,3,128]{2,0,1:T(8,128)(2,1)} %get-tuple-element.744), channel_id=1, source_target_pairs={{0,8},{8,16},{16,24},{24,32},{32,40},{40,48},{48,56},{56,64},{64,7... | collective-permute-start | bytes 884744 | tf_op jit(solution)/shard_map/while/body/eval_jaxpr/ppermute | solution.py:22
  267.4 18.0 %collective-permute-start.1 = (bf16[384,3,128]{2,0,1:T(8,128)(2,1)}, bf16[384,3,128]{2,0,1:T(8,128)(2,1)S(1)}, u32[]{:S(2)}, u32[]{:S(2)}) collective-permute-start(bf16[384,3,128]{2,0,1:T(8,128)(2,1)} %get-tuple-element.745), channel_id=1, source_target_pairs={{0,8},{8,16},{16,24},{24,32},{32,40},{40,48},{48,56},{56,64},{64,7... | collective-permute-start | bytes 884744 | tf_op jit(solution)/shard_map/while/body/eval_jaxpr/ppermute | solution.py:22
  269.3 16.1 %collective-permute-start.2 = (bf16[384,3,128]{2,0,1:T(8,128)(2,1)}, bf16[384,3,128]{2,0,1:T(8,128)(2,1)}, u32[]{:S(2)}, u32[]{:S(2)}) collective-permute-start(bf16[384,3,128]{2,0,1:T(8,128)(2,1)} %get-tuple-element.746), channel_id=1, source_target_pairs={{8,0},{16,8},{24,16},{32,24},{40,32},{48,40},{56,48},{64,56},{72,6... | collective-permute-start | bytes 884744 | tf_op jit(solution)/shard_map/while/body/eval_jaxpr/ppermute | solution.py:22
  296.2 199.8 %all-gather.3.cloned.1.call-start = ((), (), s32[]{:S(2)}) async-start(), calls=%async_computation.1 | async-start | bytes 2654208 | tf_op jit(solution)/shard_map/all_gather | solution.py:184
  507.0 55.0 %collective-permute-start.4 = (bf16[192,128]{1,0:T(8,128)(2,1)S(1)}, bf16[192,128]{1,0:T(8,128)(2,1)S(1)}, u32[]{:S(2)}, u32[]{:S(2)}) collective-permute-start(bf16[192,128]{1,0:T(8,128)(2,1)S(1)} %convert_element_type.137), channel_id=1, source_target_pairs={{0,256},{256,0},{1,257},{257,1},{2,258},{258,2},{3,259},{259,3},{4... | collective-permute-start | bytes 147464 | tf_op jit(solution)/shard_map/ppermute | solution.py:28
  (63 other events, 666.2 us)
Sparse Core Ops, SparseCore 0:
  296.3 134.7 all-reduce.2
  433.2 62.7 all-gather.2
where the time goes:
time: 623 us; the launch traced here: 619 us
  waiting for transfers between devices  195 us (31%)
  starting transfers between devices  99.6 us (16%)
  blocking collectives  95.6 us (15%)
  local copies, waits for them, and re-layouts  82.8 us (13%)
  other arithmetic  51.7 us (8%)
  loops' own time  40.7 us (7%)
  matrix products  37.7 us (6%)
  between operations  15.9 us (3%)
    psum x1, waiting for transfers between devices, local(): lax.psum(partial_out.astype(jnp.bfloat16), 'tp').astype(jnp.float32)  130 us
    ppermute x32, starting transfers between devices, from_behind(): return lax.ppermute(block, axis, route)  93.4 us
    all_gather x1, waiting for transfers between devices, local(): lax.all_gather(stream[0], 'tp', axis=1, tiled=True).astype(jnp.float32)  64.9 us
    while x64, local copies, waits for them, and re-layouts  51 us
    pmax x1, blocking collectives, local(): top_scores = lax.pmax(final_top, 'seq')  48.5 us
    psum x1, blocking collectives, local(): lax.psum((jnp.sum(hot_float * cond_square[:, None], axis=0), jnp.sum(hot_...  47.1 us
    another operation x1, loops' own time, local(): lax.fori_loop(0, reach_blocks, window_turn, (attn_state, key_rows, value_...  40.1 us
  transfers between devices with their start and end apart: 35, of which 2 were waited for; matrix products, arithmetic and copies ran while one was open for 7% of the time, Pallas kernels for 0%

commit v1 on v0

v1 whole, which is shorter than its diff:
```python
import functools
import math

import jax
import jax.numpy as jnp
import numpy as np
from jax import lax
from jax.experimental import pallas as pl
from jax.experimental.pallas import tpu as pltpu
from jax.sharding import PartitionSpec as P

MESH = pl.DeviceIdType.MESH
HDIM = 128
CH = 64
TXT = 128
STEPS = 8
NREQ = 8
PHI_MIX = 0.7
NEG = -1e30
SCALE = 1.0 / math.sqrt(float(HDIM))
EXP2_SCALE = SCALE * math.log2(math.e)
F32 = jnp.float32
BF16 = jnp.bfloat16


def frequency_row():
    pair_index = np.arange(64)
    axis_of = np.where(pair_index < 8, 0, np.where(pair_index < 36, 1, 2))
    axis_start = np.array([0, 8, 36])[axis_of]
    axis_width = np.array([16.0, 56.0, 56.0])[axis_of]
    frequency = 10000.0 ** (-2.0 * (pair_index - axis_start) / axis_width)
    return np.repeat(frequency, 2).astype(np.float32)[None, :]


def request_ends(counts):
    ends = []
    end = jnp.int32(0)
    for r in range(NREQ):
        end = end + (TXT + counts[r])
        ends.append(end)
    return ends


def pick(rows, ends, values):
    out = jnp.full(rows.shape, values[0])
    for r in range(NREQ - 1):
        out = jnp.where(rows >= ends[r], values[r + 1], out)
    return out


def prep_kernel(counts, widths, qkv_ref, freq_ref, qg_ref, kg_ref, q_ref, kv_ref, reqq_ref, reqk_ref):
    rows, heads = qkv_ref.shape[1], q_ref.shape[0]
    ends = request_ends(counts)
    starts = [jnp.int32(0)] + ends[:-1]
    row = lax.axis_index("seq") * rows + lax.broadcasted_iota(jnp.int32, (rows, HDIM), 0)
    ids = [jnp.int32(r) for r in range(NREQ)]
    reqq_ref[...] = pick(row, ends, ids)
    blocks = reqk_ref.shape[0]
    every = lax.broadcasted_iota(jnp.int32, (blocks, rows), 0) * rows + lax.broadcasted_iota(jnp.int32, (blocks, rows), 1)
    reqk_ref[...] = pick(every, ends, ids)
    start = pick(row, ends, starts)
    width = pick(row, ends, [widths[r].astype(F32) for r in range(NREQ)])
    pos = jnp.maximum(row - start - TXT, 0).astype(F32)
    height_id = jnp.floor((pos + 0.5) / width)
    width_id = pos - height_id * width
    lane = lax.broadcasted_iota(jnp.int32, (rows, HDIM), 1)
    position = jnp.where(lane < 16, 0.0, jnp.where(lane < 72, height_id, width_id))
    angle = position * freq_ref[...]
    cos = jnp.cos(angle)
    even = lane % 2 == 0
    sin = jnp.sin(angle)
    sin = jnp.where(even, -sin, sin)

    def rotated(part, h, gain):
        x = qkv_ref[part, :, h * HDIM : (h + 1) * HDIM].astype(F32)
        x = x * lax.rsqrt(jnp.mean(x * x, axis=-1, keepdims=True) + 1e-06) * gain
        partner = jnp.where(even, pltpu.roll(x, HDIM - 1, 1), pltpu.roll(x, 1, 1))
        return x * cos + partner * sin

    for h in range(heads):
        key = rotated(1, h, kg_ref[...])
        for b in range(rows // HDIM):
            span = slice(b * HDIM, (b + 1) * HDIM)
            kv_ref[h, 0, span, :] = key[span].T.astype(BF16)
        kv_ref[h, 1] = qkv_ref[2, :, h * HDIM : (h + 1) * HDIM]
        q_ref[h] = rotated(0, h, qg_ref[...]).astype(BF16)


def attend_kernel(
    q_ref, kv_ref, reqq_ref, reqk_ref, att_ref, top_ref,
    win, m_s, l_s, acc_s, right_sem, left_sem, share_sem, recv_sem,
):
    heads, rows = q_ref.shape[0], q_ref.shape[1]
    reach = win.shape[0] // 2
    me = lax.axis_index("seq")
    count = lax.axis_size("seq")
    chips = count // 2
    chip, core = me // 2, me % 2
    other = 1 - core
    right = ((chip + 1) % chips) * 2 + core
    left = ((chip + chips - 1) % chips) * 2 + core
    partner = chip * 2 + other

    barrier = pltpu.get_barrier_semaphore()
    for peer in (left, right, partner):
        pl.semaphore_signal(barrier, inc=1, device_id={"seq": peer}, device_id_type=MESH)
    pl.semaphore_wait(barrier, 3)

    def remote(src, dst, send, recv, peer):
        return pltpu.make_async_remote_copy(
            src_ref=src, dst_ref=dst, send_sem=send, recv_sem=recv,
            device_id={"seq": peer}, device_id_type=MESH,
        )

    def slot(dz, p, h):
        return win.at[dz + reach, p, h]

    def go_right(d, h, src):
        return remote(src, slot(-d, core, h), right_sem.at[d - 1, h], recv_sem.at[reach - d, core, h], right)

    def go_left(d, h, src):
        return remote(src, slot(d, core, h), left_sem.at[d - 1, h], recv_sem.at[reach + d, core, h], left)

    def share(dz, h, src):
        return remote(src, slot(dz, core, h), share_sem.at[dz + reach, h], recv_sem.at[dz + reach, core, h], partner)

    def landed(dz, p, h):
        remote(slot(dz, p, h), slot(dz, p, h), share_sem.at[0, 0], recv_sem.at[dz + reach, p, h], partner).wait_recv()

    for h in range(heads):
        go_right(1, h, kv_ref.at[h]).start()
        go_left(1, h, kv_ref.at[h]).start()
        share(0, h, kv_ref.at[h]).start()

    tiles = rows // HDIM

    def wide(x):
        return jnp.concatenate([x] * tiles, axis=1)

    def update(h, pieces):
        q = q_ref[h]
        asked = wide(reqq_ref[...])
        scores = []
        for ref, source in pieces:
            keys = jnp.concatenate([ref[0, b * HDIM : (b + 1) * HDIM, :] for b in range(tiles)], axis=1)
            s = jnp.dot(q, keys, preferred_element_type=F32)
            scores.append(jnp.where(asked == reqk_ref[pl.ds(source, 1), :], s, NEG))
        best = functools.reduce(jnp.maximum, scores)
        m_old = m_s[h]
        m_new = jnp.maximum(m_old, jnp.max(best, axis=1, keepdims=True))
        shrink = jnp.exp2((m_old - m_new) * EXP2_SCALE)
        m_wide = wide(m_new)
        total = None
        acc = acc_s[h] * shrink
        for (ref, source), s in zip(pieces, scores):
            p = jnp.exp2((s - m_wide) * EXP2_SCALE)
            total = p if total is None else total + p
            acc = acc + jnp.dot(p.astype(BF16), ref[1], preferred_element_type=F32)
        l_s[h] = l_s[h] * shrink + jnp.sum(total, axis=1, keepdims=True)
        acc_s[h] = acc
        m_s[h] = m_new

    def block_of(dz, p):
        return ((chip + dz + chips) % chips) * 2 + p

    def own(h, carry):
        m_s[h] = jnp.full((rows, HDIM), NEG, F32)
        l_s[h] = jnp.zeros((rows, HDIM), F32)
        acc_s[h] = jnp.zeros((rows, HDIM), F32)
        update(h, [(kv_ref.at[h], me)])
        return carry

    lax.fori_loop(0, heads, own, 0)

    def pair(d, p, h):
        return [(slot(-d, p, h), block_of(-d, p)), (slot(d, p, h), block_of(d, p))]

    def receive(d, h, last):
        landed(-d, core, h)
        if not last:
            go_right(d + 1, h, slot(-d, core, h)).start()
        landed(d, core, h)
        if not last:
            go_left(d + 1, h, slot(d, core, h)).start()
            share(-d, h, slot(-d, core, h)).start()
            share(d, h, slot(d, core, h)).start()

    def first(h, carry):
        receive(1, h, False)
        update(h, pair(1, core, h))
        landed(0, other, h)
        update(h, [(slot(0, other, h), partner)])
        return carry

    lax.fori_loop(0, heads, first, 0)

    def middle(t, carry):
        d = 2 + t // heads
        h = t % heads
        receive(d, h, False)
        update(h, pair(d, core, h))
        landed(1 - d, other, h)
        landed(d - 1, other, h)
        update(h, pair(d - 1, other, h))
        return carry

    lax.fori_loop(0, heads * (reach - 2), middle, 0)

    give = reach - 2 * reach * core
    take = -give

    def last(h, carry):
        landed(1 - reach, other, h)
        landed(reach - 1, other, h)
        update(h, pair(reach - 1, other, h))
        receive(reach, h, True)
        share(give, h, slot(give, core, h)).start()
        update(h, pair(reach, core, h))
        return carry

    lax.fori_loop(0, heads, last, 0)

    def ending(h, carry):
        landed(take, other, h)
        update(h, [(slot(take, other, h), block_of(take, other))])
        return carry

    lax.fori_loop(0, heads, ending, 0)

    lane = lax.broadcasted_iota(jnp.int32, (8, HDIM), 1)
    tops = jnp.zeros((8, HDIM), F32)
    for h in range(heads):
        att_ref[:, h * HDIM : (h + 1) * HDIM] = (acc_s[h] / l_s[h]).astype(BF16)
        top = jnp.max(jnp.max(m_s[h], axis=0, keepdims=True), axis=1, keepdims=True) * SCALE
        tops = jnp.where(lane == 2 * NREQ + h, top, tops)
    top_ref[...] = tops

    def drain(h, carry):
        for d in range(1, reach + 1):
            go_right(d, h, kv_ref.at[h]).wait_send()
            go_left(d, h, kv_ref.at[h]).wait_send()
        for dz in range(1 - reach, reach):
            share(dz, h, kv_ref.at[h]).wait_send()
        share(give, h, kv_ref.at[h]).wait_send()
        return carry

    lax.fori_loop(0, heads, drain, 0)


def finish_kernel(
    counts, steps, guidance, att_ref, w_ref, stream_ref, mod_ref, proj_ref, latent_ref, top_ref,
    vel_ref, next_ref, tops_ref,
    part, got, res, mixed, gate, scale, shift, flow_s, mine, flows, row_s, sums,
    part_send, part_recv, res_send, res_recv, flow_send, flow_recv, sum_send, sum_recv,
):
    n_tp, n_seq, n_cfg = lax.axis_size("tp"), lax.axis_size("seq"), lax.axis_size("cfg")
    group, me, col = lax.axis_index("cfg"), lax.axis_index("seq"), lax.axis_index("tp")
    rows, width = stream_ref.shape
    feats = w_ref.shape[1]
    piece = rows // n_tp
    barrier = pltpu.get_barrier_semaphore()

    def tp_peer(k):
        return (col + k) % n_tp

    def plane_peer(k):
        return (group + k // n_tp) % n_cfg, (col + k) % n_tp

    def seq_peer(k):
        return (me + k) % n_seq

    def hail_plane(k, carry):
        g, c = plane_peer(k)
        pl.semaphore_signal(barrier, inc=1, device_id={"cfg": g, "tp": c}, device_id_type=MESH)
        return carry

    lax.fori_loop(1, n_tp * n_cfg, hail_plane, 0)

    def hail_seq(k, carry):
        pl.semaphore_signal(barrier, inc=1, device_id={"seq": seq_peer(k)}, device_id_type=MESH)
        return carry

    lax.fori_loop(1, n_seq, hail_seq, 0)

    att = att_ref[...]
    chunk = 512

    def project(j, carry):
        at = pl.ds(pl.multiple_of(j * chunk, chunk), chunk)
        out = jnp.dot(att, w_ref[:, at], preferred_element_type=F32).astype(BF16)
        for k in range(n_tp):
            part[k, :, at] = out[k * piece : (k + 1) * piece]
        return carry

    lax.fori_loop(0, feats // chunk, project, 0)

    ends = request_ends(counts)
    token = me * rows + col * piece + lax.broadcasted_iota(jnp.int32, (piece, chunk), 0)

    def pick_rows(j, carry):
        at = pl.ds(pl.multiple_of(j * chunk, chunk), chunk)
        for which, out in ((0, gate), (1, scale), (2, shift)):
            value = jnp.broadcast_to(mod_ref[which, 0:1, at], (piece, chunk))
            for r in range(NREQ - 1):
                value = jnp.where(token >= ends[r], mod_ref[which, r + 1 : r + 2, at], value)
            out[:, at] = value
        return carry

    lax.fori_loop(0, feats // chunk, pick_rows, 0)

    pl.semaphore_wait(barrier, n_tp * n_cfg - 1 + n_seq - 1)

    def res_copy(k, dest_slot):
        c = tp_peer(k)
        return pltpu.make_async_remote_copy(
            src_ref=stream_ref.at[pl.ds(c * piece, piece)], dst_ref=res.at[dest_slot],
            send_sem=res_send.at[k], recv_sem=res_recv.at[dest_slot],
            device_id={"tp": c}, device_id_type=MESH,
        )

    def part_copy(k, dest_slot):
        c = tp_peer(k)
        return pltpu.make_async_remote_copy(
            src_ref=part.at[c], dst_ref=got.at[dest_slot],
            send_sem=part_send.at[k], recv_sem=part_recv.at[dest_slot],
            device_id={"tp": c}, device_id_type=MESH,
        )

    def give_tp(k, carry):
        res_copy(k, col).start()
        part_copy(k, col).start()
        return carry

    lax.fori_loop(1, n_tp, give_tp, 0)
    got[col] = part[col]
    res[col] = stream_ref[pl.ds(pl.multiple_of(col * piece, piece), piece), :]

    def take_tp(k, carry):
        res_copy(k, tp_peer(k)).wait_recv()
        part_copy(k, tp_peer(k)).wait_recv()
        return carry

    lax.fori_loop(1, n_tp, take_tp, 0)

    mean = jnp.zeros((piece, 1), F32)
    for j in range(n_tp):
        at = slice(j * width, (j + 1) * width)
        total = got[0, :, at].astype(F32)
        for k in range(1, n_tp):
            total = total + got[k, :, at].astype(F32)
        value = res[j].astype(F32) + gate[:, at] * total
        mixed[:, at] = value
        mean = mean + jnp.sum(value, axis=1, keepdims=True)
    mean = mean * (1.0 / feats)
    variance = jnp.zeros((piece, 1), F32)
    for j in range(n_tp):
        at = slice(j * width, (j + 1) * width)
        centred = mixed[:, at] - mean
        mixed[:, at] = centred
        variance = variance + jnp.sum(centred * centred, axis=1, keepdims=True)
    inverse = lax.rsqrt(variance * (1.0 / feats) + 1e-06)
    flow = jnp.zeros((piece, HDIM), F32)
    for j in range(n_tp):
        at = slice(j * width, (j + 1) * width)
        normed = (mixed[:, at] * inverse * (1.0 + scale[:, at]) + shift[:, at]).astype(BF16)
        flow = flow + lax.dot_general(
            normed, proj_ref[:, at], (((1,), (1,)), ((), ())), preferred_element_type=F32
        )
    flow_s[...] = flow
    even = flow_s[pl.ds(0, piece // 2, stride=2), :]
    odd = flow_s[pl.ds(1, piece // 2, stride=2), :]
    own_flow = even + pltpu.roll(odd, CH, 1)
    mine[...] = own_flow
    flows[group, col] = own_flow

    def flow_copy(k, g_slot, c_slot):
        g, c = plane_peer(k)
        return pltpu.make_async_remote_copy(
            src_ref=mine, dst_ref=flows.at[g_slot, c_slot],
            send_sem=flow_send.at[k], recv_sem=flow_recv.at[g_slot, c_slot],
            device_id={"cfg": g, "tp": c}, device_id_type=MESH,
        )

    def give_flow(k, carry):
        flow_copy(k, group, col).start()
        return carry

    lax.fori_loop(1, n_tp * n_cfg, give_flow, 0)

    pairs = rows // 2
    lane2 = lax.broadcasted_iota(jnp.int32, (pairs, HDIM), 1)
    row2 = me * rows + 2 * lax.broadcasted_iota(jnp.int32, (pairs, HDIM), 0) + (lane2 >= CH).astype(jnp.int32)
    request = pick(row2, ends, [jnp.int32(r) for r in range(NREQ)])
    image = (row2 - pick(row2, ends, [jnp.int32(0)] + ends[:-1])) >= TXT
    guide = pick(row2, ends, [guidance[r] for r in range(NREQ)])
    step = pick(row2, ends, [steps[r].astype(F32) for r in range(NREQ)])

    def sigma(u):
        remaining = 1.0 - u / STEPS
        return 3.0 * remaining / (1.0 + 2.0 * remaining)

    delta = sigma(step + 1.0) - sigma(step)

    def take_flow(k, carry):
        g, c = plane_peer(k)
        flow_copy(k, g, c).wait_recv()
        return carry

    lax.fori_loop(1, n_tp * n_cfg, take_flow, 0)

    cond = flows[0].reshape(pairs, HDIM)
    uncond = flows[1].reshape(pairs, HDIM)
    guided = uncond + guide * (cond - uncond)
    cond_square = jnp.where(image, cond * cond, 0.0)
    guided_square = jnp.where(image, guided * guided, 0.0)
    parts = []
    for square in (cond_square, guided_square):
        for r in range(NREQ):
            parts.append(jnp.sum(jnp.where(request == r, square, 0.0), axis=0, keepdims=True))
    stacked = jnp.sum(jnp.concatenate(parts, axis=0), axis=1, keepdims=True)
    diagonal = lax.broadcasted_iota(jnp.int32, (2 * NREQ, HDIM), 0) == lax.broadcasted_iota(jnp.int32, (2 * NREQ, HDIM), 1)
    own_sums = jnp.sum(jnp.where(diagonal, stacked, 0.0), axis=0, keepdims=True) + top_ref[0:1, :]
    row_s[...] = own_sums
    sums[me] = own_sums

    def sum_copy(k, dest_slot):
        return pltpu.make_async_remote_copy(
            src_ref=row_s, dst_ref=sums.at[dest_slot],
            send_sem=sum_send.at[k], recv_sem=sum_recv.at[dest_slot],
            device_id={"seq": seq_peer(k)}, device_id_type=MESH,
        )

    def give_sum(k, carry):
        sum_copy(k, me).start()
        return carry

    lax.fori_loop(1, n_seq, give_sum, 0)

    def take_sum(k, carry):
        sum_copy(k, seq_peer(k)).wait_recv()
        return carry

    lax.fori_loop(1, n_seq, take_sum, 0)

    total = sums[0]
    top = sums[0]
    for k in range(1, n_seq):
        total = total + sums[k]
        top = jnp.maximum(top, sums[k])
    tops_ref[...] = top
    lane1 = lax.broadcasted_iota(jnp.int32, (1, HDIM), 1)
    entries = jnp.ones((1, HDIM), F32)
    for r in range(NREQ):
        entries = jnp.where(lane1 == r, counts[r].astype(F32) * CH, entries)
    guided_total = pltpu.roll(total, HDIM - NREQ, 1)
    factor = (PHI_MIX * jnp.sqrt(total / entries + 1e-06) + (1.0 - PHI_MIX)) / jnp.sqrt(guided_total / entries + 1e-06)
    factor_row = jnp.zeros((pairs, HDIM), F32)
    for r in range(NREQ):
        one = jnp.sum(jnp.where(lane1 == r, factor, 0.0), axis=1, keepdims=True)
        factor_row = jnp.where(request == r, one, factor_row)
    velocity = guided * jnp.where(image, factor_row, 0.0)
    stepped = latent_ref[...] + delta * velocity
    vel_ref[...] = jnp.where(group == 0, velocity, pltpu.roll(velocity, CH, 1))
    next_ref[...] = jnp.where(group == 0, stepped, pltpu.roll(stepped, CH, 1))

    def drain_tp(k, carry):
        res_copy(k, col).wait_send()
        part_copy(k, col).wait_send()
        return carry

    lax.fori_loop(1, n_tp, drain_tp, 0)

    def drain_flow(k, carry):
        flow_copy(k, group, col).wait_send()
        return carry

    lax.fori_loop(1, n_tp * n_cfg, drain_flow, 0)

    def drain_sum(k, carry):
        sum_copy(k, me).wait_send()
        return carry

    lax.fori_loop(1, n_seq, drain_sum, 0)


def local(stream, qkv, q_gain, k_gain, w_out, mod, w_proj, latent, guidance, img_counts, img_widths, step_index):
    rows, width = stream.shape[1], stream.shape[2]
    feats = w_out.shape[1]
    heads = width // HDIM
    n_seq, n_tp, n_cfg = lax.axis_size("seq"), lax.axis_size("tp"), lax.axis_size("cfg")
    piece = rows // n_tp
    img_most = (rows * n_seq - NREQ * TXT) // 4
    reach = ((TXT + img_most + rows - 2) // rows + 1) // 2
    smem = pl.BlockSpec(memory_space=pltpu.SMEM)
    vmem = pl.BlockSpec(memory_space=pltpu.VMEM)
    dma = pltpu.SemaphoreType.DMA

    q, kv, reqq, reqk = pl.pallas_call(
        prep_kernel,
        out_shape=(
            jax.ShapeDtypeStruct((heads, rows, HDIM), BF16),
            jax.ShapeDtypeStruct((heads, 2, rows, HDIM), BF16),
            jax.ShapeDtypeStruct((rows, HDIM), jnp.int32),
            jax.ShapeDtypeStruct((n_seq, rows), jnp.int32),
        ),
        in_specs=[smem] * 2 + [vmem] * 4,
        out_specs=(vmem,) * 4,
        name="prep",
    )(
        img_counts, img_widths, jnp.transpose(qkv[0], (1, 0, 2)), jnp.asarray(frequency_row()),
        q_gain.reshape(1, HDIM), k_gain.reshape(1, HDIM),
    )

    att, top = pl.pallas_call(
        attend_kernel,
        out_shape=(
            jax.ShapeDtypeStruct((rows, width), BF16),
            jax.ShapeDtypeStruct((8, HDIM), F32),
        ),
        in_specs=[vmem] * 4,
        out_specs=(vmem,) * 2,
        scratch_shapes=[
            pltpu.VMEM((2 * reach + 1, 2, heads, 2, rows, HDIM), BF16),
            pltpu.VMEM((heads, rows, HDIM), F32),
            pltpu.VMEM((heads, rows, HDIM), F32),
            pltpu.VMEM((heads, rows, HDIM), F32),
            dma((reach, heads)),
            dma((reach, heads)),
            dma((2 * reach + 1, heads)),
            dma((2 * reach + 1, 2, heads)),
        ],
        compiler_params=pltpu.CompilerParams(collective_id=0, has_side_effects=True, vmem_limit_bytes=40 << 20),
        name="attend",
    )(q, kv, reqq, reqk)

    proj = jnp.pad(w_proj, ((0, HDIM - CH), (0, 0)))
    pairs = rows // 2
    vel, nxt, tops = pl.pallas_call(
        finish_kernel,
        out_shape=(
            jax.ShapeDtypeStruct((pairs, HDIM), F32),
            jax.ShapeDtypeStruct((pairs, HDIM), F32),
            jax.ShapeDtypeStruct((1, HDIM), F32),
        ),
        in_specs=[smem] * 3 + [vmem] * 7,
        out_specs=(vmem,) * 3,
        scratch_shapes=[
            pltpu.VMEM((n_tp, piece, feats), BF16),
            pltpu.VMEM((n_tp, piece, feats), BF16),
            pltpu.VMEM((n_tp, piece, width), BF16),
            pltpu.VMEM((piece, feats), F32),
            pltpu.VMEM((piece, feats), F32),
            pltpu.VMEM((piece, feats), F32),
            pltpu.VMEM((piece, feats), F32),
            pltpu.VMEM((piece, HDIM), F32),
            pltpu.VMEM((piece // 2, HDIM), F32),
            pltpu.VMEM((n_cfg, n_tp, piece // 2, HDIM), F32),
            pltpu.VMEM((1, HDIM), F32),
            pltpu.VMEM((n_seq, 1, HDIM), F32),
            dma((n_tp,)),
            dma((n_tp,)),
            dma((n_tp,)),
            dma((n_tp,)),
            dma((n_tp * n_cfg,)),
            dma((n_cfg, n_tp)),
            dma((n_seq,)),
            dma((n_seq,)),
        ],
        compiler_params=pltpu.CompilerParams(collective_id=1, has_side_effects=True, vmem_limit_bytes=40 << 20),
        name="finish",
    )(
        img_counts, step_index, guidance, att, w_out, stream[0], jnp.transpose(mod[0], (1, 0, 2)), proj, latent, top,
    )
    return (vel[:, :CH], nxt[:, :CH], tops[:, 2 * NREQ : 2 * NREQ + heads])


def solution(mesh):
    placed = (
        P("cfg", "seq", "tp"),
        P("cfg", "seq", None, "tp"),
        P(),
        P(),
        P("tp", None),
        P("cfg", None, None, None),
        P(),
        P("seq", None),
        P(),
        P(),
        P(),
        P(),
    )
    return jax.shard_map(
        local,
        mesh=mesh,
        in_specs=placed,
        out_specs=(P("seq", "cfg"), P("seq", "cfg"), P("cfg", "tp")),
        check_vma=False,
    )
```

time: 623 us -> 153 us (0.25)
  waiting for transfers between devices: 195 us -> 0 us
  Pallas kernels: 0 us -> 143 us
  starting transfers between devices: 99.6 us -> 0 us
  blocking collectives: 95.6 us -> 0 us
  local copies, waits for them, and re-layouts: 82.8 us -> 8.78 us
  other arithmetic: 51.7 us -> 0 us
  loops' own time: 40.7 us -> 0 us
  matrix products: 37.7 us -> 0 us
  between operations: 15.9 us -> 0.71 us
    pallas_call x0 -> x3, Pallas kernels: none -> 143 us  [the longest x1 72 us: local(): pl.pallas_call(finish_kernel, out_shape=(jax.ShapeDtypeStruct((pairs, HDI...]
    psum x1 -> x0, waiting for transfers between devices: 130 us -> none  [local(): lax.psum(partial_out.astype(jnp.bfloat16), 'tp').astype(jnp.float32)]
    ppermute x33 -> x0, starting transfers between devices: 99.3 us -> none  [the longest x32 93.4 us: from_behind(): return lax.ppermute(block, axis, route)]
    all_gather x1 -> x0, waiting for transfers between devices: 64.9 us -> none  [local(): lax.all_gather(stream[0], 'tp', axis=1, tiled=True).astype(jnp.float32)]
    while x68 -> x0, local copies, waits for them, and re-layouts: 54.4 us -> none
    pmax x1 -> x0, blocking collectives: 48.5 us -> none  [local(): top_scores = lax.pmax(final_top, 'seq')]
    psum x1 -> x0, blocking collectives: 47.1 us -> none  [local(): lax.psum((jnp.sum(hot_float * cond_square[:, None], axis=0), jnp.sum(hot_...]
    another operation x18 -> x0, loops' own time: 40.7 us -> none  [the longest x1 40.1 us: local(): lax.fori_loop(0, reach_blocks, window_turn, (attn_state, key_rows, value_...]
  transfers between devices with their start and end apart: 35 -> 0, of which waited for: 2 -> 0; matrix products, arithmetic and copies ran while one was open for 7% -> 0% of each run, Pallas kernels for 0% -> 0%
where the time goes in v1:
time: 153 us; the launch traced here: 152 us
  Pallas kernels  143 us (93%)
  local copies, waits for them, and re-layouts  8.78 us (6%)
    pallas_call x1, Pallas kernels, local(): pl.pallas_call(finish_kernel, out_shape=(jax.ShapeDtypeStruct((pairs, HDI...  72 us
    pallas_call x1, Pallas kernels, local(): pl.pallas_call(attend_kernel, out_shape=(jax.ShapeDtypeStruct((rows, widt...  66.3 us
    unnamed x24, local copies, waits for them, and re-layouts  7.15 us
    pallas_call x1, Pallas kernels, local(): pl.pallas_call(prep_kernel, out_shape=(jax.ShapeDtypeStruct((heads, rows,...  4.57 us

profile of v1, /device:TPU:1, one launch (start us, length us, event | category | flops | bytes accessed | tf_op | source)
XLA Modules:
  0.0 152.4 jit_solution(5782034391518933553)
XLA Ops:
  0.6 0.0 copy-start
  0.6 4.6 %prep.1 = (bf16[3,384,128]{2,1,0:T(8,128)(2,1)}, bf16[3,2,384,128]{3,2,1,0:T(8,128)(2,1)}, s32[384,128]{1,0:T(8,128)}, s32[32,384]{1,0:T(8,128)}) custom-call(s32[8]{0:T(128)} %counts.3, s32[8]{0:T(128)} %widths.1, bf16[3,384,384]{2,1,0:T(8,128)(2,1)} %bitcast.15, f32[1,128]{1,0:T(1,128)} %constant.5.clone.freq_ref, f32[1,128]{1,0:T(1,128)} %bitcast.16, ...), custom_call_target="tpu_custom_call" | custom-call | tf_op jit(solution)/shard_map/prep/pallas_call | solution.py:498
  5.2 0.0 copy-start.1
  5.2 1.1 copy-done.1
  6.3 0.0 copy-start.4
  6.3 1.0 copy-done.4
  7.2 0.0 copy-start.5
  7.2 0.9 copy-done.5
  8.2 0.0 copy-start.7
  8.2 0.8 copy-done.7
  9.0 66.3 %attend.1 = (bf16[384,384]{1,0:T(8,128)(2,1)S(1)}, f32[8,128]{1,0:T(8,128)S(1)}) custom-call(bf16[3,384,128]{2,1,0:T(8,128)(2,1)S(1)} %copy-done.4, bf16[3,2,384,128]{3,2,1,0:T(8,128)(2,1)S(1)} %copy-done.1, s32[384,128]{1,0:T(8,128)S(1)} %copy-done.5, s32[32,384]{1,0:T(8,128)S(1)} %copy-done.7), custom_call_target="tpu_custom_call" | custom-call | tf_op jit(solution)/shard_map/attend/pallas_call | solution.py:514
  75.3 1.1 pad.4.proj_ref
  76.4 0.0 copy-done
  76.4 0.0 copy-done.2
  76.4 0.0 copy-done.3
  76.4 0.0 copy-done.6
  76.4 0.0 copy-start.8
  76.4 0.6 copy-done.8
  77.1 0.7 copy-done.9
  77.7 0.7 copy-done.10
  78.4 72.0 %finish.1 = (f32[192,128]{1,0:T(8,128)S(1)}, f32[192,128]{1,0:T(8,128)S(1)}, f32[1,128]{1,0:T(1,128)S(1)}) custom-call(s32[8]{0:T(128)S(1)} %copy-done.8, s32[8]{0:T(128)S(1)} %copy-done.9, f32[8]{0:T(128)S(1)} %copy-done.10, bf16[384,384]{1,0:T(8,128)(2,1)S(1)} %get-tuple-element.16.att_ref, bf16[384,3072]{1,0:T(8,128)(2,1)S(1)} %copy-done, ...), custom_call_target="tpu_custom_call" | custom-call | tf_op jit(solution)/shard_map/finish/pallas_call | solution.py:538
  150.4 0.7 copy.16
  151.1 0.7 copy.17
  151.8 0.6 slice.11
  (5 shorter events, 0.0 us)
Async XLA Ops:
  0.6 75.8 %copy-start = (bf16[384,3072]{1,0:T(8,128)(2,1)S(1)}, bf16[384,3072]{1,0:T(8,128)(2,1)}, u32[]{:S(2)}) copy-start(bf16[384,3072]{1,0:T(8,128)(2,1)} %w_ref.1) | copy-start | bytes 7077892
  5.2 1.1 copy-start.1
  6.3 1.0 copy-start.4
  7.2 0.9 copy-start.5
  8.2 0.8 copy-start.7
  9.0 67.4 %copy-start.2 = (bf16[1,384,384]{2,1,0:T(8,128)(2,1)S(1)}, bf16[1,384,384]{2,1,0:T(8,128)(2,1)}, u32[]{:S(2)}) copy-start(bf16[1,384,384]{2,1,0:T(8,128)(2,1)} %param.13) | copy-start | bytes 884740
  9.0 67.4 %copy-start.3 = (f32[1,8,3,3072]{3,1,2,0:T(8,128)S(1)}, f32[1,8,3,3072]{3,1,2,0:T(8,128)}, u32[]{:S(2)}) copy-start(f32[1,8,3,3072]{3,1,2,0:T(8,128)} %param.18) | copy-start | bytes 884740
  9.0 67.4 %copy-start.6 = (f32[192,128]{1,0:T(8,128)S(1)}, f32[192,128]{1,0:T(8,128)}, u32[]{:S(2)}) copy-start(f32[192,128]{1,0:T(8,128)} %latent_ref.1) | copy-start | bytes 294916
  76.4 0.7 copy-start.8
  77.1 0.7 copy-start.9
  77.7 0.7 copy-start.10

commit v2 on v1

v2 whole, which is shorter than its diff:
```python
import functools
import math

import jax
import jax.numpy as jnp
import numpy as np
from jax import lax
from jax.experimental import pallas as pl
from jax.experimental.pallas import tpu as pltpu
from jax.sharding import PartitionSpec as P

MESH = pl.DeviceIdType.MESH
HDIM = 128
CH = 64
TXT = 128
STEPS = 8
NREQ = 8
PHI_MIX = 0.7
NEG = -1e30
SCALE = 1.0 / math.sqrt(float(HDIM))
EXP2_SCALE = SCALE * math.log2(math.e)
F32 = jnp.float32
BF16 = jnp.bfloat16


def frequency_row():
    pair_index = np.arange(64)
    axis_of = np.where(pair_index < 8, 0, np.where(pair_index < 36, 1, 2))
    axis_start = np.array([0, 8, 36])[axis_of]
    axis_width = np.array([16.0, 56.0, 56.0])[axis_of]
    frequency = 10000.0 ** (-2.0 * (pair_index - axis_start) / axis_width)
    return np.repeat(frequency, 2).astype(np.float32)[None, :]


def request_ends(counts):
    ends = []
    end = jnp.int32(0)
    for r in range(NREQ):
        end = end + (TXT + counts[r])
        ends.append(end)
    return ends


def pick(rows, ends, values):
    out = jnp.full(rows.shape, values[0])
    for r in range(NREQ - 1):
        out = jnp.where(rows >= ends[r], values[r + 1], out)
    return out


ORDER = ((1, 0), (1, 1), (2, 0), (2, 1), (3, 0), (1, 2), (3, 1), (4, 0), (2, 2), (4, 1), (3, 2), (4, 2))
D_CODE = sum(d * 5**i for i, (d, h) in enumerate(ORDER))
H_CODE = sum(h * 3**i for i, (d, h) in enumerate(ORDER))


def kernel(
    counts, widths, steps, guidance, qkv_ref, w_ref, stream_ref, mod_ref, proj_ref, latent_ref, freq_ref, qg_ref, kg_ref,
    vel_ref, next_ref, tops_ref,
    qkv, q_s, kv, reqq, reqk, win, m_s, l_s, acc_s,
    wall, att_s, attx, made, yout, ygot,
    res, mod_s, proj_s, mixed, gate, scale, shift, flow_s, mine, flows, row_s, sums,
    load_sem, right_sem, left_sem, share_sem, recv_sem, wsend, wrecv, wshare, wpartner,
    att_send, att_recv, y_send, y_recv, res_send, res_recv, flow_send, flow_recv, sum_send, sum_recv,
):
    n_tp, n_seq, n_cfg = lax.axis_size("tp"), lax.axis_size("seq"), lax.axis_size("cfg")
    group, me, col = lax.axis_index("cfg"), lax.axis_index("seq"), lax.axis_index("tp")
    heads, rows = q_s.shape[0], q_s.shape[1]
    width = heads * HDIM
    feats = w_ref.shape[1]
    half = feats // 2
    piece = rows // n_tp
    quarter = 2 * piece
    reach = win.shape[0] // 2
    chips = n_seq // 2
    chip, core = me // 2, me % 2
    other = 1 - core
    right = ((chip + 1) % chips) * 2 + core
    left = ((chip + chips - 1) % chips) * 2 + core
    partner = chip * 2 + other
    n_x = n_tp // 2
    tx, ty = col // 2, col % 2
    tiles = rows // HDIM
    barrier = pltpu.get_barrier_semaphore()

    def tp_peer(k):
        return (col + k) % n_tp

    def plane_peer(k):
        return (group + k // n_tp) % n_cfg, (col + k) % n_tp

    def seq_peer(k):
        return (me + k) % n_seq

    def hail_plane(k, carry):
        g, c = plane_peer(k)
        pl.semaphore_signal(barrier, inc=1, device_id={"cfg": g, "tp": c}, device_id_type=MESH)
        return carry

    lax.fori_loop(1, n_tp * n_cfg, hail_plane, 0)

    def hail_seq(k, carry):
        pl.semaphore_signal(barrier, inc=1, device_id={"seq": seq_peer(k)}, device_id_type=MESH)
        return carry

    lax.fori_loop(1, n_seq, hail_seq, 0)

    def remote(src, dst, send, recv, axis, peer):
        return pltpu.make_async_remote_copy(
            src_ref=src, dst_ref=dst, send_sem=send, recv_sem=recv,
            device_id={axis: peer}, device_id_type=MESH,
        )

    loads = [
        pltpu.make_async_copy(qkv_ref.at[1], qkv.at[1], load_sem.at[0]),
        pltpu.make_async_copy(qkv_ref.at[0], qkv.at[0], load_sem.at[1]),
        pltpu.make_async_copy(mod_ref, mod_s, load_sem.at[2]),
        pltpu.make_async_copy(proj_ref, proj_s.at[pl.ds(0, CH)], load_sem.at[3]),
        pltpu.make_async_copy(stream_ref.at[pl.ds(pl.multiple_of(col * piece, piece), piece)], res.at[col], load_sem.at[4]),
    ]
    for copy in loads:
        copy.start()
    values = [
        pltpu.make_async_copy(qkv_ref.at[2, :, pl.ds(h * HDIM, HDIM)], kv.at[h, 1], load_sem.at[5 + h]) for h in range(heads)
    ]
    for copy in values:
        copy.start()
    my_cols = pl.ds(pl.multiple_of(ty * half, half), half)
    near_cols = pl.ds(pl.multiple_of((1 - ty) * half, half), half)
    own_w = pltpu.make_async_copy(w_ref.at[:, my_cols], wall.at[col], load_sem.at[5 + heads])
    own_w.start()

    ends = request_ends(counts)
    starts = [jnp.int32(0)] + ends[:-1]
    ids = [jnp.int32(r) for r in range(NREQ)]
    row = me * rows + lax.broadcasted_iota(jnp.int32, (rows, HDIM), 0)
    start = pick(row, ends, starts)
    span = pick(row, ends, [widths[r].astype(F32) for r in range(NREQ)])
    pos = jnp.maximum(row - start - TXT, 0).astype(F32)
    height_id = jnp.floor((pos + 0.5) / span)
    width_id = pos - height_id * span
    lane = lax.broadcasted_iota(jnp.int32, (rows, HDIM), 1)
    angle = jnp.where(lane < 16, 0.0, jnp.where(lane < 72, height_id, width_id)) * freq_ref[...]
    even = lane % 2 == 0
    cos = jnp.cos(angle)
    sin = jnp.sin(angle)
    sin = jnp.where(even, -sin, sin)

    def rotated(part, h, gain):
        x = qkv[part, :, h * HDIM : (h + 1) * HDIM].astype(F32)
        x = x * lax.rsqrt(jnp.mean(x * x, axis=-1, keepdims=True) + 1e-06) * gain
        mate = jnp.where(even, pltpu.roll(x, HDIM - 1, 1), pltpu.roll(x, 1, 1))
        return x * cos + mate * sin

    loads[0].wait()
    for h in range(heads):
        key = rotated(1, h, kg_ref[...])
        for b in range(tiles):
            at = slice(b * HDIM, (b + 1) * HDIM)
            kv[h, 0, at, :] = key[at].T.astype(BF16)
    for copy in values:
        copy.wait()

    pl.semaphore_wait(barrier, n_tp * n_cfg - 1 + n_seq - 1)

    def slot(dz, p, h):
        return win.at[dz + reach, p, h]

    def go_right(d, h, src):
        return remote(src, slot(-d, core, h), right_sem.at[d - 1, h], recv_sem.at[reach - d, core, h], "seq", right)

    def go_left(d, h, src):
        return remote(src, slot(d, core, h), left_sem.at[d - 1, h], recv_sem.at[reach + d, core, h], "seq", left)

    def share(dz, h, src):
        return remote(src, slot(dz, core, h), share_sem.at[dz + reach, h], recv_sem.at[dz + reach, core, h], "seq", partner)

    def landed(dz, p, h):
        remote(slot(dz, p, h), slot(dz, p, h), share_sem.at[0, 0], recv_sem.at[dz + reach, p, h], "seq", partner).wait_recv()

    def set_out(h):
        go_right(1, h, kv.at[h]).start()
        go_left(1, h, kv.at[h]).start()
        share(0, h, kv.at[h]).start()

    set_out(0)
    set_out(1)

    x_next = ((tx + 1) % n_x) * 2 + ty
    x_prev = ((tx + n_x - 1) % n_x) * 2 + ty
    y_peer = tx * 2 + 1 - ty
    far_x = ((tx + 2) % n_x) * 2
    core_rows = pl.ds(pl.multiple_of(core * 2 * quarter, 2 * quarter), 2 * quarter)
    low_rows = pl.ds(pl.multiple_of(core * 2 * quarter, quarter), quarter)
    high_rows = pl.ds(pl.multiple_of(core * 2 * quarter + quarter, quarter), quarter)
    mate_rows = pl.ds(pl.multiple_of(other * 2 * quarter, 2 * quarter), 2 * quarter)
    mate_low = pl.ds(pl.multiple_of(other * 2 * quarter, quarter), quarter)
    mate_high = pl.ds(pl.multiple_of(other * 2 * quarter + quarter, quarter), quarter)

    def w_at(source, part):
        return wall.at[source, part]

    prev_own, prev_near = x_prev, (x_prev // 2) * 2 + 1 - ty
    next_own, next_near = x_next, (x_next // 2) * 2 + 1 - ty
    far_own, far_near = far_x + ty, far_x + 1 - ty
    pieces = [
        (y_peer, core_rows, mate_rows),
        (prev_own, core_rows, mate_rows),
        (prev_near, core_rows, mate_rows),
        (next_own, core_rows, mate_rows),
        (next_near, core_rows, mate_rows),
        (far_own, low_rows, mate_low),
        (far_near, low_rows, mate_low),
        (far_own, high_rows, mate_high),
        (far_near, high_rows, mate_high),
    ]

    def w_sends():
        own = w_ref.at[core_rows, my_cols]
        near = w_at(y_peer, core_rows)
        return [
            remote(w_ref.at[core_rows, near_cols], w_at(col, core_rows), wsend.at[0], wrecv.at[0], "tp", y_peer),
            remote(own, w_at(col, core_rows), wsend.at[1], wrecv.at[1], "tp", x_next),
            remote(own, w_at(col, core_rows), wsend.at[3], wrecv.at[3], "tp", x_prev),
            remote(near, near, wsend.at[2], wrecv.at[2], "tp", x_next),
            remote(near, near, wsend.at[4], wrecv.at[4], "tp", x_prev),
            remote(w_at(prev_own, low_rows), w_at(prev_own, low_rows), wsend.at[5], wrecv.at[5], "tp", x_next),
            remote(w_at(next_own, high_rows), w_at(next_own, high_rows), wsend.at[7], wrecv.at[7], "tp", x_prev),
            remote(w_at(prev_near, low_rows), w_at(prev_near, low_rows), wsend.at[6], wrecv.at[6], "tp", x_next),
            remote(w_at(next_near, high_rows), w_at(next_near, high_rows), wsend.at[8], wrecv.at[8], "tp", x_prev),
        ]

    w_out = w_sends()

    def w_share(n):
        source, part, _ = pieces[n]
        return remote(w_at(source, part), w_at(source, part), wshare.at[n], wpartner.at[n], "seq", partner)

    def w_landed(n):
        source, part, _ = pieces[n]
        remote(w_at(source, part), w_at(source, part), wshare.at[n], wrecv.at[n], "tp", y_peer).wait_recv()

    def w_shared(n):
        source, _, part = pieces[n]
        remote(w_at(source, part), w_at(source, part), wshare.at[n], wpartner.at[n], "seq", partner).wait_recv()

    for n in (0, 1, 2):
        w_out[n].start()

    def res_copy(k, dest_slot):
        c = tp_peer(k)
        return remote(
            stream_ref.at[pl.ds(pl.multiple_of(c * piece, piece), piece)], res.at[dest_slot],
            res_send.at[k], res_recv.at[dest_slot], "tp", c,
        )

    def give_res(k, carry):
        res_copy(k, col).start()
        return carry

    lax.fori_loop(1, n_tp, give_res, 0)

    loads[1].wait()
    for h in range(heads):
        q_s[h] = rotated(0, h, qg_ref[...]).astype(BF16)
    reqq[...] = pick(row, ends, ids)
    every = lax.broadcasted_iota(jnp.int32, (n_seq, rows), 0) * rows + lax.broadcasted_iota(jnp.int32, (n_seq, rows), 1)
    reqk[...] = pick(every, ends, ids)

    def wide(x):
        return jnp.concatenate([x] * tiles, axis=1)

    def update(h, blocks):
        q = q_s[h]
        asked = wide(reqq[...])
        scores = []
        for ref, source in blocks:
            keys = jnp.concatenate([ref[0, b * HDIM : (b + 1) * HDIM, :] for b in range(tiles)], axis=1)
            s = jnp.dot(q, keys, preferred_element_type=F32)
            scores.append(jnp.where(asked == reqk[pl.ds(source, 1), :], s, NEG))
        best = functools.reduce(jnp.maximum, scores)
        m_old = m_s[h]
        m_new = jnp.maximum(m_old, jnp.max(best, axis=1, keepdims=True))
        shrink = jnp.exp2((m_old - m_new) * EXP2_SCALE)
        m_wide = wide(m_new)
        total = None
        acc = acc_s[h] * shrink
        for (ref, source), s in zip(blocks, scores):
            p = jnp.exp2((s - m_wide) * EXP2_SCALE)
            total = p if total is None else total + p
            acc = acc + jnp.dot(p.astype(BF16), ref[1], preferred_element_type=F32)
        l_s[h] = l_s[h] * shrink + jnp.sum(total, axis=1, keepdims=True)
        acc_s[h] = acc
        m_s[h] = m_new

    def block_of(dz, p):
        return ((chip + dz + chips) % chips) * 2 + p

    def own(h, carry):
        m_s[h] = jnp.full((rows, HDIM), NEG, F32)
        l_s[h] = jnp.zeros((rows, HDIM), F32)
        acc_s[h] = jnp.zeros((rows, HDIM), F32)
        update(h, [(kv.at[h], me)])
        return carry

    lax.fori_loop(0, heads, own, 0)

    loads[2].wait()
    chunk = 512
    token = me * rows + col * piece + lax.broadcasted_iota(jnp.int32, (piece, chunk), 0)

    def pick_rows(j, carry):
        at = pl.ds(pl.multiple_of(j * chunk, chunk), chunk)
        for which, out in ((0, gate), (1, scale), (2, shift)):
            value = jnp.broadcast_to(mod_s[which, 0:1, at], (piece, chunk))
            for r in range(NREQ - 1):
                value = jnp.where(token >= ends[r], mod_s[which, r + 1 : r + 2, at], value)
            out[:, at] = value
        return carry

    lax.fori_loop(0, feats // chunk, pick_rows, 0)

    give = reach - 2 * reach * core
    take = -give

    def pair(d, p, h):
        return [(slot(-d, p, h), block_of(-d, p)), (slot(d, p, h), block_of(d, p))]

    def att_copy(h, k, dest_slot):
        c = tp_peer(k)
        return remote(
            att_s.at[h, pl.ds(pl.multiple_of((c // 2) * quarter, quarter), quarter)], attx.at[h, dest_slot],
            att_send.at[h, k], att_recv.at[h, dest_slot], "tp", c,
        )

    def give_att(h):
        att_s[h] = (acc_s[h] / l_s[h]).astype(BF16)

        def one(k, carry):
            att_copy(h, k, col).start()
            return carry

        lax.fori_loop(1, n_tp, one, 0)
        attx[h, col] = att_s[h, pl.ds(pl.multiple_of(tx * quarter, quarter), quarter), :]

    def take_att(h):
        def one(k, carry):
            att_copy(h, k, tp_peer(k)).wait_recv()
            return carry

        lax.fori_loop(1, n_tp, one, 0)

    def product(h, at):
        left_side = jnp.concatenate([attx[h, k] for k in range(n_tp)], axis=1)
        weights = wall[:, h * HDIM : (h + 1) * HDIM, at].reshape(n_tp * HDIM, chunk)
        return jnp.dot(left_side, weights, preferred_element_type=F32)

    def step(i, carry):
        d_code, h_code, d_last, h_last = carry
        d, h = d_code % 5, h_code % 3

        @pl.when(i == 3)
        def _():
            w_landed(0)
            w_out[3].start()
            w_out[4].start()
            w_landed(1)
            w_out[5].start()
            w_landed(3)
            w_out[6].start()
            for n in (0, 1, 3):
                w_share(n).start()

        @pl.when(i == 7)
        def _():
            w_landed(2)
            w_out[7].start()
            w_landed(4)
            w_out[8].start()
            for n in (2, 4):
                w_share(n).start()

        @pl.when(i == 9)
        def _():
            for n in (5, 7):
                w_landed(n)
                w_share(n).start()

        @pl.when(i == 11)
        def _():
            take_att(1)

            def one(j, c):
                at = pl.ds(pl.multiple_of(j * chunk, chunk), chunk)
                made[:, at] = made[:, at] + product(1, at)
                return c

            lax.fori_loop(0, half // chunk, one, 0)

        landed(-d, core, h)

        @pl.when(d < reach)
        def _():
            go_right(d + 1, h, slot(-d, core, h)).start()

        landed(d, core, h)

        @pl.when(d < reach)
        def _():
            go_left(d + 1, h, slot(d, core, h)).start()
            share(-d, h, slot(-d, core, h)).start()
            share(d, h, slot(d, core, h)).start()

        @pl.when(d == reach)
        def _():
            share(give, h, slot(give, core, h)).start()

        @pl.when(i == 2)
        def _():
            set_out(2)

        update(h, pair(d, core, h))

        @pl.when((i > 0) & (d_last < reach))
        def _():
            landed(-d_last, other, h_last)
            landed(d_last, other, h_last)
            update(h_last, pair(d_last, other, h_last))

        @pl.when(((i > 0) & (i < 4)) | (d_last == reach))
        def _():
            near = (d_last != reach).astype(jnp.int32)
            dz = (1 - near) * take
            hh = near * (i - 1) + (1 - near) * h_last
            landed(dz, other, hh)
            update(hh, [(slot(dz, other, hh), block_of(dz, other))])

        @pl.when(i == 8)
        def _():
            give_att(0)

        @pl.when(i == 10)
        def _():
            give_att(1)
            for n in (6, 8):
                w_landed(n)
                w_share(n).start()
            own_w.wait()
            for n in range(9):
                w_shared(n)
            take_att(0)

            def one(j, c):
                at = pl.ds(pl.multiple_of(j * chunk, chunk), chunk)
                made[:, at] = product(0, at)
                return c

            lax.fori_loop(0, half // chunk, one, 0)

        return d_code // 5, h_code // 3, d, h

    lax.fori_loop(0, len(ORDER), step, (jnp.int32(D_CODE), jnp.int32(H_CODE), jnp.int32(0), jnp.int32(0)))

    landed(take, other, 2)
    update(2, [(slot(take, other, 2), block_of(take, other))])
    give_att(2)

    lane8 = lax.broadcasted_iota(jnp.int32, (1, HDIM), 1)
    top_row = jnp.zeros((1, HDIM), F32)
    for h in range(heads):
        top = jnp.max(jnp.max(m_s[h], axis=0, keepdims=True), axis=1, keepdims=True) * SCALE
        top_row = jnp.where(lane8 == 2 * NREQ + h, top, top_row)

    loads[3].wait()
    proj_s[pl.ds(CH, HDIM - CH), :] = jnp.zeros((HDIM - CH, feats), BF16)
    loads[4].wait()

    def take_res(k, carry):
        res_copy(k, tp_peer(k)).wait_recv()
        return carry

    lax.fori_loop(1, n_tp, take_res, 0)
    take_att(2)

    def y_copy(j):
        return remote(yout.at[j], ygot.at[j], y_send.at[j], y_recv.at[j], "tp", y_peer)

    keep = pl.ds(pl.multiple_of(ty * piece, piece), piece)
    pass_on = pl.ds(pl.multiple_of((1 - ty) * piece, piece), piece)

    def last_product(j, carry):
        at = pl.ds(pl.multiple_of(j * chunk, chunk), chunk)
        made[:, at] = made[:, at] + product(2, at)
        yout[j] = made[pass_on, at].astype(BF16)
        y_copy(j).start()
        return carry

    lax.fori_loop(0, half // chunk, last_product, 0)

    total1 = jnp.zeros((piece, 1), F32)
    for j in range(half // width):
        at = pl.ds(pl.multiple_of(ty * half + j * width, width), width)
        value = res[ty * (n_tp // 2) + j].astype(F32) + gate[:, at] * made[keep, j * width : (j + 1) * width]
        mixed[:, at] = value
        total1 = total1 + jnp.sum(value, axis=1, keepdims=True)
    for j in range(half // chunk):
        y_copy(j).wait_recv()
        at = pl.ds(pl.multiple_of((1 - ty) * half + j * chunk, chunk), chunk)
        mixed[:, at] = gate[:, at] * ygot[j].astype(F32)
    for j in range(half // width):
        at = pl.ds(pl.multiple_of((1 - ty) * half + j * width, width), width)
        value = res[(1 - ty) * (n_tp // 2) + j].astype(F32) + mixed[:, at]
        mixed[:, at] = value
        total1 = total1 + jnp.sum(value, axis=1, keepdims=True)
    mean = total1 * (1.0 / feats)
    variance = jnp.zeros((piece, 1), F32)
    for j in range(n_tp):
        at = slice(j * width, (j + 1) * width)
        centred = mixed[:, at] - mean
        mixed[:, at] = centred
        variance = variance + jnp.sum(centred * centred, axis=1, keepdims=True)
    inverse = lax.rsqrt(variance * (1.0 / feats) + 1e-06)
    flow = jnp.zeros((piece, HDIM), F32)
    for j in range(n_tp):
        at = slice(j * width, (j + 1) * width)
        normed = (mixed[:, at] * inverse * (1.0 + scale[:, at]) + shift[:, at]).astype(BF16)
        flow = flow + lax.dot_general(
            normed, proj_s[:, at], (((1,), (1,)), ((), ())), preferred_element_type=F32
        )
    flow_s[...] = flow
    even_rows = flow_s[pl.ds(0, piece // 2, stride=2), :]
    odd_rows = flow_s[pl.ds(1, piece // 2, stride=2), :]
    own_flow = even_rows + pltpu.roll(odd_rows, CH, 1)
    mine[...] = own_flow
    flows[group, col] = own_flow
    def flow_copy(k, g_slot, c_slot):
        g, c = plane_peer(k)
        return pltpu.make_async_remote_copy(
            src_ref=mine, dst_ref=flows.at[g_slot, c_slot],
            send_sem=flow_send.at[k], recv_sem=flow_recv.at[g_slot, c_slot],
            device_id={"cfg": g, "tp": c}, device_id_type=MESH,
        )

    def give_flow(k, carry):
        flow_copy(k, group, col).start()
        return carry

    lax.fori_loop(1, n_tp * n_cfg, give_flow, 0)

    pairs = rows // 2
    lane2 = lax.broadcasted_iota(jnp.int32, (pairs, HDIM), 1)
    row2 = me * rows + 2 * lax.broadcasted_iota(jnp.int32, (pairs, HDIM), 0) + (lane2 >= CH).astype(jnp.int32)
    request = pick(row2, ends, [jnp.int32(r) for r in range(NREQ)])
    image = (row2 - pick(row2, ends, [jnp.int32(0)] + ends[:-1])) >= TXT
    guide = pick(row2, ends, [guidance[r] for r in range(NREQ)])
    at_step = pick(row2, ends, [steps[r].astype(F32) for r in range(NREQ)])

    def sigma(u):
        remaining = 1.0 - u / STEPS
        return 3.0 * remaining / (1.0 + 2.0 * remaining)

    delta = sigma(at_step + 1.0) - sigma(at_step)

    def take_flow(k, carry):
        g, c = plane_peer(k)
        flow_copy(k, g, c).wait_recv()
        return carry

    lax.fori_loop(1, n_tp * n_cfg, take_flow, 0)

    cond = flows[0].reshape(pairs, HDIM)
    uncond = flows[1].reshape(pairs, HDIM)
    guided = uncond + guide * (cond - uncond)
    cond_square = jnp.where(image, cond * cond, 0.0)
    guided_square = jnp.where(image, guided * guided, 0.0)
    parts = []
    for square in (cond_square, guided_square):
        for r in range(NREQ):
            parts.append(jnp.sum(jnp.where(request == r, square, 0.0), axis=0, keepdims=True))
    stacked = jnp.sum(jnp.concatenate(parts, axis=0), axis=1, keepdims=True)
    diagonal = lax.broadcasted_iota(jnp.int32, (2 * NREQ, HDIM), 0) == lax.broadcasted_iota(jnp.int32, (2 * NREQ, HDIM), 1)
    own_sums = jnp.sum(jnp.where(diagonal, stacked, 0.0), axis=0, keepdims=True) + top_row
    row_s[...] = own_sums
    sums[me] = own_sums

    def sum_copy(k, dest_slot):
        return pltpu.make_async_remote_copy(
            src_ref=row_s, dst_ref=sums.at[dest_slot],
            send_sem=sum_send.at[k], recv_sem=sum_recv.at[dest_slot],
            device_id={"seq": seq_peer(k)}, device_id_type=MESH,
        )

    def give_sum(k, carry):
        sum_copy(k, me).start()
        return carry

    lax.fori_loop(1, n_seq, give_sum, 0)

    def take_sum(k, carry):
        sum_copy(k, seq_peer(k)).wait_recv()
        return carry

    lax.fori_loop(1, n_seq, take_sum, 0)

    total = sums[0]
    top = sums[0]
    for k in range(1, n_seq):
        total = total + sums[k]
        top = jnp.maximum(top, sums[k])
    tops_ref[...] = top
    lane1 = lax.broadcasted_iota(jnp.int32, (1, HDIM), 1)
    entries = jnp.ones((1, HDIM), F32)
    for r in range(NREQ):
        entries = jnp.where(lane1 == r, counts[r].astype(F32) * CH, entries)
    guided_total = pltpu.roll(total, HDIM - NREQ, 1)
    factor = (PHI_MIX * jnp.sqrt(total / entries + 1e-06) + (1.0 - PHI_MIX)) / jnp.sqrt(guided_total / entries + 1e-06)
    factor_row = jnp.zeros((pairs, HDIM), F32)
    for r in range(NREQ):
        one = jnp.sum(jnp.where(lane1 == r, factor, 0.0), axis=1, keepdims=True)
        factor_row = jnp.where(request == r, one, factor_row)
    velocity = guided * jnp.where(image, factor_row, 0.0)
    stepped = latent_ref[...] + delta * velocity
    vel_ref[...] = jnp.where(group == 0, velocity, pltpu.roll(velocity, CH, 1))
    next_ref[...] = jnp.where(group == 0, stepped, pltpu.roll(stepped, CH, 1))

    def drain_tp(k, carry):
        res_copy(k, col).wait_send()
        for h in range(heads):
            att_copy(h, k, col).wait_send()
        return carry

    lax.fori_loop(1, n_tp, drain_tp, 0)

    def drain_flow(k, carry):
        flow_copy(k, group, col).wait_send()
        return carry

    lax.fori_loop(1, n_tp * n_cfg, drain_flow, 0)

    def drain_sum(k, carry):
        sum_copy(k, me).wait_send()
        return carry

    lax.fori_loop(1, n_seq, drain_sum, 0)

    def drain(h, carry):
        for d in range(1, reach + 1):
            go_right(d, h, kv.at[h]).wait_send()
            go_left(d, h, kv.at[h]).wait_send()
        for dz in range(1 - reach, reach):
            share(dz, h, kv.at[h]).wait_send()
        share(give, h, kv.at[h]).wait_send()
        return carry

    lax.fori_loop(0, heads, drain, 0)
    for copy in w_out:
        copy.wait_send()
    for n in range(9):
        w_share(n).wait_send()
    for j in range(half // chunk):
        y_copy(j).wait_send()


def local(stream, qkv, q_gain, k_gain, w_out, mod, w_proj, latent, guidance, img_counts, img_widths, step_index):
    rows, width = stream.shape[1], stream.shape[2]
    feats = w_out.shape[1]
    heads = width // HDIM
    n_seq, n_tp, n_cfg = lax.axis_size("seq"), lax.axis_size("tp"), lax.axis_size("cfg")
    piece = rows // n_tp
    img_most = (rows * n_seq - NREQ * TXT) // 4
    reach = ((TXT + img_most + rows - 2) // rows + 1) // 2
    smem = pl.BlockSpec(memory_space=pltpu.SMEM)
    vmem = pl.BlockSpec(memory_space=pltpu.VMEM)
    hbm = pl.BlockSpec(memory_space=pl.ANY)
    dma = pltpu.SemaphoreType.DMA
    pairs = rows // 2
    half = feats // 2
    chunk = 512
    vel, nxt, tops = pl.pallas_call(
        kernel,
        out_shape=(
            jax.ShapeDtypeStruct((pairs, HDIM), F32),
            jax.ShapeDtypeStruct((pairs, HDIM), F32),
            jax.ShapeDtypeStruct((1, HDIM), F32),
        ),
        in_specs=[smem] * 4 + [hbm] * 5 + [vmem] * 4,
        out_specs=(vmem,) * 3,
        scratch_shapes=[
            pltpu.VMEM((2, rows, width), BF16),
            pltpu.VMEM((heads, rows, HDIM), BF16),
            pltpu.VMEM((heads, 2, rows, HDIM), BF16),
            pltpu.VMEM((rows, HDIM), jnp.int32),
            pltpu.VMEM((n_seq, rows), jnp.int32),
            pltpu.VMEM((2 * reach + 1, 2, heads, 2, rows, HDIM), BF16),
            pltpu.VMEM((heads, rows, HDIM), F32),
            pltpu.VMEM((heads, rows, HDIM), F32),
            pltpu.VMEM((heads, rows, HDIM), F32),
            pltpu.VMEM((n_tp, rows, half), BF16),
            pltpu.VMEM((heads, rows, HDIM), BF16),
            pltpu.VMEM((heads, n_tp, 2 * piece, HDIM), BF16),
            pltpu.VMEM((2 * piece, half), F32),
            pltpu.VMEM((half // chunk, piece, chunk), BF16),
            pltpu.VMEM((half // chunk, piece, chunk), BF16),
            pltpu.VMEM((n_tp, piece, width), BF16),
            pltpu.VMEM((3, NREQ, feats), F32),
            pltpu.VMEM((HDIM, feats), BF16),
            pltpu.VMEM((piece, feats), F32),
            pltpu.VMEM((piece, feats), F32),
            pltpu.VMEM((piece, feats), F32),
            pltpu.VMEM((piece, feats), F32),
            pltpu.VMEM((piece, HDIM), F32),
            pltpu.VMEM((piece // 2, HDIM), F32),
            pltpu.VMEM((n_cfg, n_tp, piece // 2, HDIM), F32),
            pltpu.VMEM((1, HDIM), F32),
            pltpu.VMEM((n_seq, 1, HDIM), F32),
            dma((6 + heads,)),
            dma((reach, heads)),
            dma((reach, heads)),
            dma((2 * reach + 1, heads)),
            dma((2 * reach + 1, 2, heads)),
            dma((9,)),
            dma((9,)),
            dma((9,)),
            dma((9,)),
            dma((heads, n_tp)),
            dma((heads, n_tp)),
            dma((half // chunk,)),
            dma((half // chunk,)),
            dma((n_tp,)),
            dma((n_tp,)),
            dma((n_tp * n_cfg,)),
            dma((n_cfg, n_tp)),
            dma((n_seq,)),
            dma((n_seq,)),
        ],
        compiler_params=pltpu.CompilerParams(collective_id=0, has_side_effects=True, vmem_limit_bytes=56 << 20),
        name="flow_step",
    )(
        img_counts, img_widths, step_index, guidance, jnp.transpose(qkv[0], (1, 0, 2)), w_out, stream[0],
        jnp.transpose(mod[0], (1, 0, 2)), w_proj, latent, jnp.asarray(frequency_row()),
        q_gain.reshape(1, HDIM), k_gain.reshape(1, HDIM),
    )
    return (vel[:, :CH], nxt[:, :CH], tops[:, 2 * NREQ : 2 * NREQ + heads])


def solution(mesh):
    placed = (
        P("cfg", "seq", "tp"),
        P("cfg", "seq", None, "tp"),
        P(),
        P(),
        P("tp", None),
        P("cfg", None, None, None),
        P(),
        P("seq", None),
        P(),
        P(),
        P(),
        P(),
    )
    return jax.shard_map(
        local,
        mesh=mesh,
        in_specs=placed,
        out_specs=(P("seq", "cfg"), P("seq", "cfg"), P("cfg", "tp")),
        check_vma=False,
    )
```

time: 153 us -> 110 us (0.72)
  Pallas kernels: 143 us -> 105 us
  local copies, waits for them, and re-layouts: 8.78 us -> 4.41 us
    pallas_call x3 -> x1, Pallas kernels: 143 us -> 105 us  [local(): pl.pallas_call(kernel, out_shape=(jax.ShapeDtypeStruct((pairs, HDIM), F32...]
    unnamed x24 -> x2, local copies, waits for them, and re-layouts: 7.15 us -> 3.21 us
where the time goes in v2:
time: 110 us
  Pallas kernels  105 us (95%)
  local copies, waits for them, and re-layouts  4.41 us (4%)
    pallas_call x1, Pallas kernels, local(): pl.pallas_call(kernel, out_shape=(jax.ShapeDtypeStruct((pairs, HDIM), F32...  105 us
    unnamed x2, local copies, waits for them, and re-layouts  3.21 us

profile of v2, /device:TPU:1, one launch (start us, length us, event | category | flops | bytes accessed | tf_op | source)
XLA Modules:
  0.0 109.8 jit_solution(15092788909272560969)
XLA Ops:
  0.6 104.7 %flow_step.1 = (f32[192,128]{1,0:T(8,128)}, f32[192,128]{1,0:T(8,128)}, f32[1,128]{1,0:T(1,128)}) custom-call(s32[8]{0:T(128)} %counts.1, s32[8]{0:T(128)} %widths.1, s32[8]{0:T(128)} %steps.1, f32[8]{0:T(128)} %guidance.1, bf16[3,384,384]{2,1,0:T(8,128)(2,1)} %bitcast.11, bf16[384,3072]{1,0:T(8,128)(2,1)} %w_ref.1, bf16[384,384]{1,0:T(8,128)(2,1)} %bitcast.12, ...), custom_call_target="tpu_custom_call" | custom-call | tf_op jit(solution)/shard_map/flow_step/pallas_call | solution.py:678
  105.4 1.6 %copy.16 = f32[192,64]{0,1:T(8,128)} copy(f32[192,64]{1,0:T(8,128)} %bitcast.15) | data formatting | bytes 98304
  107.0 1.6 %copy.17 = f32[192,64]{0,1:T(8,128)} copy(f32[192,64]{1,0:T(8,128)} %bitcast.14) | data formatting | bytes 98304
  108.6 1.2 %slice.11 = f32[1,3]{1,0:T(1,128)} slice(f32[1,128]{1,0:T(1,128)} %get-tuple-element.8), slice={[0:1], [16:19]} | slice | bytes 24 | tf_op jit(solution)/shard_map/slice | solution.py:742

commit v3 on v2

--- a/solution.py
+++ b/solution.py
@@ -54,12 +54,14 @@
 
 
 def kernel(
-    counts, widths, steps, guidance, qkv_ref, w_ref, stream_ref, mod_ref, proj_ref, latent_ref, freq_ref, qg_ref, kg_ref,
+    rim,
+    counts_ref, widths_ref, steps_ref, guidance_ref, qkv_ref, w_ref, stream_ref, mod_ref, proj_ref, latent_ref,
+    freq_ref, qg_ref, kg_ref,
     vel_ref, next_ref, tops_ref,
-    qkv, q_s, kv, reqq, reqk, win, m_s, l_s, acc_s,
+    counts, widths, steps, guidance, latent_s, freq_s, qg_s, kg_s, qkv, q_s, kv, reqq, reqk, win, m_s, l_s, acc_s,
     wall, att_s, attx, made, yout, ygot,
     res, mod_s, proj_s, mixed, gate, scale, shift, flow_s, mine, flows, row_s, sums,
-    load_sem, right_sem, left_sem, share_sem, recv_sem, wsend, wrecv, wshare, wpartner,
+    first_sem, load_sem, right_sem, left_sem, share_sem, recv_sem, wsend, wrecv, wshare, wpartner,
     att_send, att_recv, y_send, y_recv, res_send, res_recv, flow_send, flow_recv, sum_send, sum_recv,
 ):
     n_tp, n_seq, n_cfg = lax.axis_size("tp"), lax.axis_size("seq"), lax.axis_size("cfg")
@@ -98,11 +100,18 @@
 
     lax.fori_loop(1, n_tp * n_cfg, hail_plane, 0)
 
+    near_count = 4 * reach + 1
+
     def hail_seq(k, carry):
-        pl.semaphore_signal(barrier, inc=1, device_id={"seq": seq_peer(k)}, device_id_type=MESH)
-        return carry
-
-    lax.fori_loop(1, n_seq, hail_seq, 0)
+        peer = (2 * chip + 2 * n_seq - 2 * reach + k) % n_seq
+
+        @pl.when(peer != me)
+        def _():
+            pl.semaphore_signal(barrier, inc=1, device_id={"seq": peer}, device_id_type=MESH)
+
+        return carry
+
+    lax.fori_loop(0, near_count + 1, hail_seq, 0)
 
     def remote(src, dst, send, recv, axis, peer):
         return pltpu.make_async_remote_copy(
@@ -110,6 +119,17 @@
             device_id={axis: peer}, device_id_type=MESH,
         )
 
+    firsts = [
+        pltpu.make_async_copy(source, target, first_sem.at[n])
+        for n, (source, target) in enumerate(
+            (
+                (counts_ref, counts), (widths_ref, widths), (steps_ref, steps), (guidance_ref, guidance),
+                (freq_ref, freq_s), (qg_ref, qg_s), (kg_ref, kg_s), (latent_ref, latent_s),
+            )
+        )
+    ]
+    for copy in firsts:
+        copy.start()
     loads = [
         pltpu.make_async_copy(qkv_ref.at[1], qkv.at[1], load_sem.at[0]),
         pltpu.make_async_copy(qkv_ref.at[0], qkv.at[0], load_sem.at[1]),
@@ -129,6 +149,8 @@
     own_w = pltpu.make_async_copy(w_ref.at[:, my_cols], wall.at[col], load_sem.at[5 + heads])
     own_w.start()
 
+    for copy in firsts:
+        copy.wait()
     ends = request_ends(counts)
     starts = [jnp.int32(0)] + ends[:-1]
     ids = [jnp.int32(r) for r in range(NREQ)]
@@ -139,7 +161,7 @@
     height_id = jnp.floor((pos + 0.5) / span)
     width_id = pos - height_id * span
     lane = lax.broadcasted_iota(jnp.int32, (rows, HDIM), 1)
-    angle = jnp.where(lane < 16, 0.0, jnp.where(lane < 72, height_id, width_id)) * freq_ref[...]
+    angle = jnp.where(lane < 16, 0.0, jnp.where(lane < 72, height_id, width_id)) * freq_s[...]
     even = lane % 2 == 0
     cos = jnp.cos(angle)
     sin = jnp.sin(angle)
@@ -151,17 +173,17 @@
         mate = jnp.where(even, pltpu.roll(x, HDIM - 1, 1), pltpu.roll(x, 1, 1))
         return x * cos + mate * sin
 
-    loads[0].wait()
-    for h in range(heads):
-        key = rotated(1, h, kg_ref[...])
+    def make_key(h):
+        key = rotated(1, h, kg_s[...])
         for b in range(tiles):
             at = slice(b * HDIM, (b + 1) * HDIM)
             kv[h, 0, at, :] = key[at].T.astype(BF16)
+
+    loads[0].wait()
+    make_key(0)
     for copy in values:
         copy.wait()
 
-    pl.semaphore_wait(barrier, n_tp * n_cfg - 1 + n_seq - 1)
-
     def slot(dz, p, h):
         return win.at[dz + reach, p, h]
 
@@ -176,13 +198,41 @@
 
     def landed(dz, p, h):
         remote(slot(dz, p, h), slot(dz, p, h), share_sem.at[0, 0], recv_sem.at[dz + reach, p, h], "seq", partner).wait_recv()
+
+    cut = rows - rim
+    whole, early, late = pl.ds(0, rows), pl.ds(0, rim), pl.ds(cut, rim)
+
+    def rim_right(h, at):
+        return remote(
+            slot(1 - reach, core, h).at[:, at], slot(-reach, core, h).at[:, at],
+            right_sem.at[reach - 1, h], recv_sem.at[0, core, h], "seq", right,
+        )
+
+    def rim_left(h, at):
+        return remote(
+            slot(reach - 1, core, h).at[:, at], slot(reach, core, h).at[:, at],
+            left_sem.at[reach - 1, h], recv_sem.at[2 * reach, core, h], "seq", left,
+        )
+
+    def at_rim(right_op, left_op):
+        @pl.when(core == 0)
+        def _():
+            right_op(late)
+            left_op(whole)
+
+        @pl.when(core == 1)
+        def _():
+            right_op(whole)
+            left_op(early)
 
     def set_out(h):
         go_right(1, h, kv.at[h]).start()
         go_left(1, h, kv.at[h]).start()
         share(0, h, kv.at[h]).start()
 
+    pl.semaphore_wait(barrier, n_tp * n_cfg - 1 + near_count)
     set_out(0)
+    make_key(1)
     set_out(1)
 
     x_next = ((tx + 1) % n_x) * 2 + ty
@@ -259,9 +309,10 @@
 
     lax.fori_loop(1, n_tp, give_res, 0)
 
+    make_key(2)
     loads[1].wait()
     for h in range(heads):
-        q_s[h] = rotated(0, h, qg_ref[...]).astype(BF16)
+        q_s[h] = rotated(0, h, qg_s[...]).astype(BF16)
     reqq[...] = pick(row, ends, ids)
     every = lax.broadcasted_iota(jnp.int32, (n_seq, rows), 0) * rows + lax.broadcasted_iota(jnp.int32, (n_seq, rows), 1)
     reqk[...] = pick(every, ends, ids)
@@ -296,6 +347,16 @@
         return ((chip + dz + chips) % chips) * 2 + p
 
     def own(h, carry):
+        blank = jnp.zeros((2, cut, HDIM), BF16)
+
+        @pl.when(core == 0)
+        def _():
+            win[0, 0, h, :, pl.ds(0, cut), :] = blank
+
+        @pl.when(core == 1)
+        def _():
+            win[2 * reach, 1, h, :, pl.ds(rim, cut), :] = blank
+
         m_s[h] = jnp.full((rows, HDIM), NEG, F32)
         l_s[h] = jnp.zeros((rows, HDIM), F32)
         acc_s[h] = jnp.zeros((rows, HDIM), F32)
@@ -396,22 +457,27 @@
 
             lax.fori_loop(0, half // chunk, one, 0)
 
-        landed(-d, core, h)
+        @pl.when(d < reach - 1)
+        def _():
+            landed(-d, core, h)
+            go_right(d + 1, h, slot(-d, core, h)).start()
+            landed(d, core, h)
+            go_left(d + 1, h, slot(d, core, h)).start()
+
+        @pl.when(d == reach - 1)
+        def _():
+            landed(-d, core, h)
+            landed(d, core, h)
+            at_rim(lambda at: rim_right(h, at).start(), lambda at: rim_left(h, at).start())
 
         @pl.when(d < reach)
         def _():
-            go_right(d + 1, h, slot(-d, core, h)).start()
-
-        landed(d, core, h)
-
-        @pl.when(d < reach)
-        def _():
-            go_left(d + 1, h, slot(d, core, h)).start()
             share(-d, h, slot(-d, core, h)).start()
             share(d, h, slot(d, core, h)).start()
 
         @pl.when(d == reach)
         def _():
+            at_rim(lambda at: rim_right(h, at).wait_recv(), lambda at: rim_left(h, at).wait_recv())
             share(give, h, slot(give, core, h)).start()
 
         @pl.when(i == 2)
@@ -606,7 +672,7 @@
     for k in range(1, n_seq):
         total = total + sums[k]
         top = jnp.maximum(top, sums[k])
-    tops_ref[...] = top
+    tops_ref[...] = pltpu.roll(top, HDIM - 2 * NREQ, 1)[:, :heads]
     lane1 = lax.broadcasted_iota(jnp.int32, (1, HDIM), 1)
     entries = jnp.ones((1, HDIM), F32)
     for r in range(NREQ):
@@ -618,9 +684,11 @@
         one = jnp.sum(jnp.where(lane1 == r, factor, 0.0), axis=1, keepdims=True)
         factor_row = jnp.where(request == r, one, factor_row)
     velocity = guided * jnp.where(image, factor_row, 0.0)
-    stepped = latent_ref[...] + delta * velocity
-    vel_ref[...] = jnp.where(group == 0, velocity, pltpu.roll(velocity, CH, 1))
-    next_ref[...] = jnp.where(group == 0, stepped, pltpu.roll(stepped, CH, 1))
+    stepped = latent_s[...] + delta * velocity
+    for value, out in ((velocity, vel_ref), (stepped, next_ref)):
+        value = jnp.where(group == 0, value, pltpu.roll(value, CH, 1))
+        out[:, :HDIM] = value[:HDIM].T[:CH]
+        out[:, HDIM:] = jnp.concatenate([value[HDIM:], value[HDIM:]], axis=0).T[:CH, : pairs - HDIM]
 
     def drain_tp(k, carry):
         res_copy(k, col).wait_send()
@@ -643,9 +711,10 @@
     lax.fori_loop(1, n_seq, drain_sum, 0)
 
     def drain(h, carry):
-        for d in range(1, reach + 1):
+        for d in range(1, reach):
             go_right(d, h, kv.at[h]).wait_send()
             go_left(d, h, kv.at[h]).wait_send()
+        at_rim(lambda at: rim_right(h, at).wait_send(), lambda at: rim_left(h, at).wait_send())
         for dz in range(1 - reach, reach):
             share(dz, h, kv.at[h]).wait_send()
         share(give, h, kv.at[h]).wait_send()
@@ -667,8 +736,9 @@
     n_seq, n_tp, n_cfg = lax.axis_size("seq"), lax.axis_size("tp"), lax.axis_size("cfg")
     piece = rows // n_tp
     img_most = (rows * n_seq - NREQ * TXT) // 4
-    reach = ((TXT + img_most + rows - 2) // rows + 1) // 2
-    smem = pl.BlockSpec(memory_space=pltpu.SMEM)
+    longest = TXT + img_most
+    reach = ((longest + rows - 2) // rows + 1) // 2
+    rim = min(rows, -(-(longest - (2 * reach - 1) * rows - 1) // HDIM) * HDIM)
     vmem = pl.BlockSpec(memory_space=pltpu.VMEM)
     hbm = pl.BlockSpec(memory_space=pl.ANY)
     dma = pltpu.SemaphoreType.DMA
@@ -676,15 +746,23 @@
     half = feats // 2
     chunk = 512
     vel, nxt, tops = pl.pallas_call(
-        kernel,
+        functools.partial(kernel, rim),
         out_shape=(
-            jax.ShapeDtypeStruct((pairs, HDIM), F32),
-            jax.ShapeDtypeStruct((pairs, HDIM), F32),
-            jax.ShapeDtypeStruct((1, HDIM), F32),
+            jax.ShapeDtypeStruct((CH, pairs), F32),
+            jax.ShapeDtypeStruct((CH, pairs), F32),
+            jax.ShapeDtypeStruct((1, heads), F32),
         ),
-        in_specs=[smem] * 4 + [hbm] * 5 + [vmem] * 4,
+        in_specs=[hbm] * 13,
         out_specs=(vmem,) * 3,
         scratch_shapes=[
+            pltpu.SMEM((NREQ,), jnp.int32),
+            pltpu.SMEM((NREQ,), jnp.int32),
+            pltpu.SMEM((NREQ,), jnp.int32),
+            pltpu.SMEM((NREQ,), F32),
+            pltpu.VMEM((pairs, HDIM), F32),
+            pltpu.VMEM((1, HDIM), F32),
+            pltpu.VMEM((1, HDIM), F32),
+            pltpu.VMEM((1, HDIM), F32),
             pltpu.VMEM((2, rows, width), BF16),
             pltpu.VMEM((heads, rows, HDIM), BF16),
             pltpu.VMEM((heads, 2, rows, HDIM), BF16),
@@ -712,6 +790,7 @@
             pltpu.VMEM((n_cfg, n_tp, piece // 2, HDIM), F32),
             pltpu.VMEM((1, HDIM), F32),
             pltpu.VMEM((n_seq, 1, HDIM), F32),
+            dma((8,)),
             dma((6 + heads,)),
             dma((reach, heads)),
             dma((reach, heads)),
@@ -739,7 +818,7 @@
         jnp.transpose(mod[0], (1, 0, 2)), w_proj, latent, jnp.asarray(frequency_row()),
         q_gain.reshape(1, HDIM), k_gain.reshape(1, HDIM),
     )
-    return (vel[:, :CH], nxt[:, :CH], tops[:, 2 * NREQ : 2 * NREQ + heads])
+    return (vel.T, nxt.T, tops)
 
 
 def solution(mesh):

time: 110 us -> 106 us (0.964)
  Pallas kernels: 105 us -> 101 us
    pallas_call x1, Pallas kernels: 105 us -> 101 us  [local(): pl.pallas_call(functools.partial(kernel, rim), out_shape=(jax.ShapeDtypeS...]
    slice x1 -> x0, local copies, waits for them, and re-layouts: 1.2 us -> none  [local(): return (vel[:, :CH], nxt[:, :CH], tops[:, 2 * NREQ:2 * NREQ + heads])]
    unnamed x2 -> x3, local copies, waits for them, and re-layouts: 3.21 us -> 4.12 us
where the time goes in v3:
time: 106 us; the launch traced here: 105 us
  Pallas kernels  101 us (95%)
  local copies, waits for them, and re-layouts  4.12 us (4%)
    pallas_call x1, Pallas kernels, local(): pl.pallas_call(functools.partial(kernel, rim), out_shape=(jax.ShapeDtypeS...  101 us
    unnamed x3, local copies, waits for them, and re-layouts  4.12 us

profile of v3, /device:TPU:1, one launch (start us, length us, event | category | flops | bytes accessed | tf_op | source)
XLA Modules:
  0.0 105.3 jit_solution(10317319212487544815)
XLA Ops:
  0.6 100.6 %flow_step.1 = (f32[64,192]{1,0:T(8,128)}, f32[64,192]{1,0:T(8,128)}, f32[1,3]{1,0:T(1,128)}) custom-call(s32[8]{0:T(128)} %counts_ref.1, s32[8]{0:T(128)} %widths_ref.1, s32[8]{0:T(128)} %steps_ref.1, f32[8]{0:T(128)} %guidance_ref.1, bf16[3,384,384]{2,1,0:T(8,128)(2,1)} %bitcast.11, bf16[384,3072]{1,0:T(8,128)(2,1)} %w_ref.1, bf16[384,384]{1,0:T(8,128)(2,1)} %bitcast.12, ...), custom_call_target="tpu_custom_call" | custom-call | tf_op jit(solution)/shard_map/flow_step/pallas_call | solution.py:748
  101.2 1.5 %copy.19 = f32[192,64]{0,1:T(8,128)} copy(f32[192,64]{0,1:T(8,128)} %bitcast.15) | data formatting | bytes 98304
  102.7 1.5 %copy.20 = f32[192,64]{0,1:T(8,128)} copy(f32[192,64]{0,1:T(8,128)} %bitcast.14) | data formatting | bytes 98304
  104.2 1.2 %copy.21 = f32[1,3]{1,0:T(1,128)} copy(f32[1,3]{1,0:T(1,128)} %get-tuple-element.14) | data formatting | bytes 24

commit v4 on v3

--- a/solution.py
+++ b/solution.py
@@ -46,11 +46,6 @@
     for r in range(NREQ - 1):
         out = jnp.where(rows >= ends[r], values[r + 1], out)
     return out
-
-
-ORDER = ((1, 0), (1, 1), (2, 0), (2, 1), (3, 0), (1, 2), (3, 1), (4, 0), (2, 2), (4, 1), (3, 2), (4, 2))
-D_CODE = sum(d * 5**i for i, (d, h) in enumerate(ORDER))
-H_CODE = sum(h * 3**i for i, (d, h) in enumerate(ORDER))
 
 
 def kernel(
@@ -234,6 +229,8 @@
     set_out(0)
     make_key(1)
     set_out(1)
+    make_key(2)
+    set_out(2)
 
     x_next = ((tx + 1) % n_x) * 2 + ty
     x_prev = ((tx + n_x - 1) % n_x) * 2 + ty
@@ -309,7 +306,6 @@
 
     lax.fori_loop(1, n_tp, give_res, 0)
 
-    make_key(2)
     loads[1].wait()
     for h in range(heads):
         q_s[h] = rotated(0, h, qg_s[...]).astype(BF16)
@@ -416,8 +412,8 @@
         return jnp.dot(left_side, weights, preferred_element_type=F32)
 
     def step(i, carry):
-        d_code, h_code, d_last, h_last = carry
-        d, h = d_code % 5, h_code % 3
+        d, h = 1 + i // heads, i % heads
+        d_last, h_last = 1 + (i + heads - 1) // heads - 1, (i + heads - 1) % heads
 
         @pl.when(i == 3)
         def _():
@@ -446,17 +442,6 @@
                 w_landed(n)
                 w_share(n).start()
 
-        @pl.when(i == 11)
-        def _():
-            take_att(1)
-
-            def one(j, c):
-                at = pl.ds(pl.multiple_of(j * chunk, chunk), chunk)
-                made[:, at] = made[:, at] + product(1, at)
-                return c
-
-            lax.fori_loop(0, half // chunk, one, 0)
-
         @pl.when(d < reach - 1)
         def _():
             landed(-d, core, h)
@@ -479,10 +464,6 @@
         def _():
             at_rim(lambda at: rim_right(h, at).wait_recv(), lambda at: rim_left(h, at).wait_recv())
             share(give, h, slot(give, core, h)).start()
-
-        @pl.when(i == 2)
-        def _():
-            set_out(2)
 
         update(h, pair(d, core, h))
 
@@ -500,35 +481,37 @@
             landed(dz, other, hh)
             update(hh, [(slot(dz, other, hh), block_of(dz, other))])
 
-        @pl.when(i == 8)
-        def _():
-            give_att(0)
-
         @pl.when(i == 10)
         def _():
-            give_att(1)
             for n in (6, 8):
                 w_landed(n)
                 w_share(n).start()
-            own_w.wait()
-            for n in range(9):
-                w_shared(n)
-            take_att(0)
-
-            def one(j, c):
-                at = pl.ds(pl.multiple_of(j * chunk, chunk), chunk)
-                made[:, at] = product(0, at)
-                return c
-
-            lax.fori_loop(0, half // chunk, one, 0)
-
-        return d_code // 5, h_code // 3, d, h
-
-    lax.fori_loop(0, len(ORDER), step, (jnp.int32(D_CODE), jnp.int32(H_CODE), jnp.int32(0), jnp.int32(0)))
-
-    landed(take, other, 2)
-    update(2, [(slot(take, other, 2), block_of(take, other))])
-    give_att(2)
+
+        for done in range(heads - 1):
+
+            @pl.when(i == heads * (reach - 1) + done + 1)
+            def _():
+                give_att(done)
+
+        return carry
+
+    lax.fori_loop(0, heads * reach, step, 0)
+
+    landed(take, other, heads - 1)
+    update(heads - 1, [(slot(take, other, heads - 1), block_of(take, other))])
+    give_att(heads - 1)
+    own_w.wait()
+    for n in range(9):
+        w_shared(n)
+    take_att(0)
+    take_att(1)
+
+    def early_product(j, carry):
+        at = pl.ds(pl.multiple_of(j * chunk, chunk), chunk)
+        made[:, at] = product(0, at) + product(1, at)
+        return carry
+
+    lax.fori_loop(0, half // chunk, early_product, 0)
 
     lane8 = lax.broadcasted_iota(jnp.int32, (1, HDIM), 1)
     top_row = jnp.zeros((1, HDIM), F32)
@@ -740,7 +723,7 @@
     reach = ((longest + rows - 2) // rows + 1) // 2
     rim = min(rows, -(-(longest - (2 * reach - 1) * rows - 1) // HDIM) * HDIM)
     vmem = pl.BlockSpec(memory_space=pltpu.VMEM)
-    hbm = pl.BlockSpec(memory_space=pl.ANY)
+    hbm = pl.BlockSpec(memory_space=pltpu.HBM)
     dma = pltpu.SemaphoreType.DMA
     pairs = rows // 2
     half = feats // 2
@@ -811,13 +794,13 @@
             dma((n_seq,)),
             dma((n_seq,)),
         ],
-        compiler_params=pltpu.CompilerParams(collective_id=0, has_side_effects=True, vmem_limit_bytes=56 << 20),
+        compiler_params=pltpu.CompilerParams(collective_id=0, has_side_effects=True, vmem_limit_bytes=38 << 20),
         name="flow_step",
-    )(
+    )(*(pltpu.with_memory_space_constraint(x, pltpu.HBM) for x in (
         img_counts, img_widths, step_index, guidance, jnp.transpose(qkv[0], (1, 0, 2)), w_out, stream[0],
         jnp.transpose(mod[0], (1, 0, 2)), w_proj, latent, jnp.asarray(frequency_row()),
         q_gain.reshape(1, HDIM), k_gain.reshape(1, HDIM),
-    )
+    )))
     return (vel.T, nxt.T, tops)
 
 

time: 106 us -> 100 us (0.943)
  Pallas kernels: 101 us -> 97.9 us
  local copies, waits for them, and re-layouts: 4.12 us -> 1.77 us
    pallas_call x1, Pallas kernels: 101 us -> 97.9 us  [local(): pl.pallas_call(functools.partial(kernel, rim), out_shape=(jax.ShapeDtypeS...]
    unnamed x3, local copies, waits for them, and re-layouts: 4.12 us -> 1.77 us
where the time goes in v4:
time: 100 us
  Pallas kernels  97.9 us (98%)
  local copies, waits for them, and re-layouts  1.77 us (2%)
    pallas_call x1, Pallas kernels, local(): pl.pallas_call(functools.partial(kernel, rim), out_shape=(jax.ShapeDtypeS...  97.9 us

profile of v4, /device:TPU:1, one launch (start us, length us, event | category | flops | bytes accessed | tf_op | source)
XLA Modules:
  0.0 100.4 jit_solution(13687175494777002406)
XLA Ops:
  0.6 97.9 %flow_step.1 = (f32[64,192]{1,0:T(8,128)S(1)}, f32[64,192]{1,0:T(8,128)S(1)}, f32[1,3]{1,0:T(1,128)S(1)}) custom-call(s32[8]{0:T(128)} %counts_ref.1, s32[8]{0:T(128)} %widths_ref.1, s32[8]{0:T(128)} %steps_ref.1, f32[8]{0:T(128)} %guidance_ref.1, bf16[3,384,384]{2,1,0:T(8,128)(2,1)} %bitcast.13, bf16[384,3072]{1,0:T(8,128)(2,1)} %w_ref.1, ...), custom_call_target="tpu_custom_call" | custom-call | tf_op jit(solution)/shard_map/flow_step/pallas_call | solution.py:731
  98.6 0.6 copy.19
  99.2 0.6 copy.20
  99.8 0.5 copy.21

commit v5 on v4

--- a/solution.py
+++ b/solution.py
@@ -411,6 +411,23 @@
         weights = wall[:, h * HDIM : (h + 1) * HDIM, at].reshape(n_tp * HDIM, chunk)
         return jnp.dot(left_side, weights, preferred_element_type=F32)
 
+    def multiply(h):
+        def one(j, carry):
+            at = pl.ds(pl.multiple_of(j * chunk, chunk), chunk)
+            made[:, at] = product(h, at) if h == 0 else made[:, at] + product(h, at)
+            return carry
+
+        lax.fori_loop(0, half // chunk, one, 0)
+
+    def from_partner(d, h):
+        landed(-d, other, h)
+        landed(d, other, h)
+        update(h, pair(d, other, h))
+
+    def one_from_partner(dz, h):
+        landed(dz, other, h)
+        update(h, [(slot(dz, other, h), block_of(dz, other))])
+
     def step(i, carry):
         d, h = 1 + i // heads, i % heads
         d_last, h_last = 1 + (i + heads - 1) // heads - 1, (i + heads - 1) % heads
@@ -442,6 +459,27 @@
                 w_landed(n)
                 w_share(n).start()
 
+        @pl.when(i == heads * (reach - 1))
+        def _():
+            from_partner(d_last, h_last)
+
+        for done in range(heads - 1):
+
+            @pl.when(i == heads * (reach - 1) + done + 1)
+            def _():
+                one_from_partner(take, done)
+                give_att(done)
+                if done == 0:
+                    for n in (6, 8):
+                        w_landed(n)
+                        w_share(n).start()
+                else:
+                    own_w.wait()
+                    for n in range(9):
+                        w_shared(n)
+                    take_att(0)
+                    multiply(0)
+
         @pl.when(d < reach - 1)
         def _():
             landed(-d, core, h)
@@ -467,51 +505,22 @@
 
         update(h, pair(d, core, h))
 
-        @pl.when((i > 0) & (d_last < reach))
-        def _():
-            landed(-d_last, other, h_last)
-            landed(d_last, other, h_last)
-            update(h_last, pair(d_last, other, h_last))
-
-        @pl.when(((i > 0) & (i < 4)) | (d_last == reach))
-        def _():
-            near = (d_last != reach).astype(jnp.int32)
-            dz = (1 - near) * take
-            hh = near * (i - 1) + (1 - near) * h_last
-            landed(dz, other, hh)
-            update(hh, [(slot(dz, other, hh), block_of(dz, other))])
-
-        @pl.when(i == 10)
-        def _():
-            for n in (6, 8):
-                w_landed(n)
-                w_share(n).start()
-
-        for done in range(heads - 1):
-
-            @pl.when(i == heads * (reach - 1) + done + 1)
-            def _():
-                give_att(done)
+        @pl.when((i > 0) & (d < reach))
+        def _():
+            from_partner(d_last, h_last)
+
+        @pl.when((i > 0) & (i < 4))
+        def _():
+            one_from_partner(0, i - 1)
 
         return carry
 
     lax.fori_loop(0, heads * reach, step, 0)
 
-    landed(take, other, heads - 1)
-    update(heads - 1, [(slot(take, other, heads - 1), block_of(take, other))])
+    one_from_partner(take, heads - 1)
     give_att(heads - 1)
-    own_w.wait()
-    for n in range(9):
-        w_shared(n)
-    take_att(0)
     take_att(1)
-
-    def early_product(j, carry):
-        at = pl.ds(pl.multiple_of(j * chunk, chunk), chunk)
-        made[:, at] = product(0, at) + product(1, at)
-        return carry
-
-    lax.fori_loop(0, half // chunk, early_product, 0)
+    multiply(1)
 
     lane8 = lax.broadcasted_iota(jnp.int32, (1, HDIM), 1)
     top_row = jnp.zeros((1, HDIM), F32)

time: 100 us -> 101 us (1.010)
  no operation moved by 1% of the time
where the time goes in v5:
time: 101 us
  Pallas kernels  98.9 us (98%)
  local copies, waits for them, and re-layouts  1.77 us (2%)
    pallas_call x1, Pallas kernels, local(): pl.pallas_call(functools.partial(kernel, rim), out_shape=(jax.ShapeDtypeS...  98.9 us

profile of v5, /device:TPU:1, one launch (start us, length us, event | category | flops | bytes accessed | tf_op | source)
XLA Modules:
  0.0 101.3 jit_solution(292674525919893420)
XLA Ops:
  0.6 98.9 %flow_step.1 = (f32[64,192]{1,0:T(8,128)S(1)}, f32[64,192]{1,0:T(8,128)S(1)}, f32[1,3]{1,0:T(1,128)S(1)}) custom-call(s32[8]{0:T(128)} %counts_ref.1, s32[8]{0:T(128)} %widths_ref.1, s32[8]{0:T(128)} %steps_ref.1, f32[8]{0:T(128)} %guidance_ref.1, bf16[3,384,384]{2,1,0:T(8,128)(2,1)} %bitcast.13, bf16[384,3072]{1,0:T(8,128)(2,1)} %w_ref.1, ...), custom_call_target="tpu_custom_call" | custom-call | tf_op jit(solution)/shard_map/flow_step/pallas_call | solution.py:740
  99.6 0.6 copy.19
  100.2 0.6 copy.20
  100.8 0.5 copy.21

commit v6 on v5

--- a/solution.py
+++ b/solution.py
@@ -411,14 +411,6 @@
         weights = wall[:, h * HDIM : (h + 1) * HDIM, at].reshape(n_tp * HDIM, chunk)
         return jnp.dot(left_side, weights, preferred_element_type=F32)
 
-    def multiply(h):
-        def one(j, carry):
-            at = pl.ds(pl.multiple_of(j * chunk, chunk), chunk)
-            made[:, at] = product(h, at) if h == 0 else made[:, at] + product(h, at)
-            return carry
-
-        lax.fori_loop(0, half // chunk, one, 0)
-
     def from_partner(d, h):
         landed(-d, other, h)
         landed(d, other, h)
@@ -473,12 +465,6 @@
                     for n in (6, 8):
                         w_landed(n)
                         w_share(n).start()
-                else:
-                    own_w.wait()
-                    for n in range(9):
-                        w_shared(n)
-                    take_att(0)
-                    multiply(0)
 
         @pl.when(d < reach - 1)
         def _():
@@ -519,8 +505,18 @@
 
     one_from_partner(take, heads - 1)
     give_att(heads - 1)
+    own_w.wait()
+    for n in range(9):
+        w_shared(n)
+    take_att(0)
     take_att(1)
-    multiply(1)
+
+    def early_product(j, carry):
+        at = pl.ds(pl.multiple_of(j * chunk, chunk), chunk)
+        made[:, at] = product(0, at) + product(1, at)
+        return carry
+
+    lax.fori_loop(0, half // chunk, early_product, 0)
 
     lane8 = lax.broadcasted_iota(jnp.int32, (1, HDIM), 1)
     top_row = jnp.zeros((1, HDIM), F32)

time: 101 us -> 97.9 us (0.969)
  Pallas kernels: 98.9 us -> 95.3 us
    pallas_call x1, Pallas kernels: 98.9 us -> 95.3 us  [local(): pl.pallas_call(functools.partial(kernel, rim), out_shape=(jax.ShapeDtypeS...]
where the time goes in v6:
time: 97.9 us; the launch traced here: 97.8 us
  Pallas kernels  95.3 us (97%)
  local copies, waits for them, and re-layouts  1.77 us (2%)
    pallas_call x1, Pallas kernels, local(): pl.pallas_call(functools.partial(kernel, rim), out_shape=(jax.ShapeDtypeS...  95.3 us

profile of v6, /device:TPU:1, one launch (start us, length us, event | category | flops | bytes accessed | tf_op | source)
XLA Modules:
  0.0 97.8 jit_solution(3720285690896071721)
XLA Ops:
  0.6 95.3 %flow_step.1 = (f32[64,192]{1,0:T(8,128)S(1)}, f32[64,192]{1,0:T(8,128)S(1)}, f32[1,3]{1,0:T(1,128)S(1)}) custom-call(s32[8]{0:T(128)} %counts_ref.1, s32[8]{0:T(128)} %widths_ref.1, s32[8]{0:T(128)} %steps_ref.1, f32[8]{0:T(128)} %guidance_ref.1, bf16[3,384,384]{2,1,0:T(8,128)(2,1)} %bitcast.13, bf16[384,3072]{1,0:T(8,128)(2,1)} %w_ref.1, ...), custom_call_target="tpu_custom_call" | custom-call | tf_op jit(solution)/shard_map/flow_step/pallas_call | solution.py:736
  96.0 0.6 copy.19
  96.6 0.6 copy.20
  97.2 0.5 copy.21

commit v7 on v6

--- a/solution.py
+++ b/solution.py
@@ -82,6 +82,9 @@
     def tp_peer(k):
         return (col + k) % n_tp
 
+    def far_first(t, count):
+        return count // 2 + (t + 1) // 2 * (1 - 2 * (t % 2))
+
     def plane_peer(k):
         return (group + k // n_tp) % n_cfg, (col + k) % n_tp
 
@@ -93,8 +96,6 @@
         pl.semaphore_signal(barrier, inc=1, device_id={"cfg": g, "tp": c}, device_id_type=MESH)
         return carry
 
-    lax.fori_loop(1, n_tp * n_cfg, hail_plane, 0)
-
     near_count = 4 * reach + 1
 
     def hail_seq(k, carry):
@@ -107,6 +108,7 @@
         return carry
 
     lax.fori_loop(0, near_count + 1, hail_seq, 0)
+    lax.fori_loop(1, n_tp * n_cfg, hail_plane, 0)
 
     def remote(src, dst, send, recv, axis, peer):
         return pltpu.make_async_remote_copy(
@@ -392,11 +394,11 @@
     def give_att(h):
         att_s[h] = (acc_s[h] / l_s[h]).astype(BF16)
 
-        def one(k, carry):
-            att_copy(h, k, col).start()
+        def one(t, carry):
+            att_copy(h, far_first(t, n_tp), col).start()
             return carry
 
-        lax.fori_loop(1, n_tp, one, 0)
+        lax.fori_loop(0, n_tp - 1, one, 0)
         attx[h, col] = att_s[h, pl.ds(pl.multiple_of(tx * quarter, quarter), quarter), :]
 
     def take_att(h):
@@ -594,11 +596,12 @@
             device_id={"cfg": g, "tp": c}, device_id_type=MESH,
         )
 
-    def give_flow(k, carry):
+    def give_flow(t, carry):
+        k = (1 - t % 2) * n_tp + far_first(t // 2, n_tp)
         flow_copy(k, group, col).start()
         return carry
 
-    lax.fori_loop(1, n_tp * n_cfg, give_flow, 0)
+    lax.fori_loop(0, n_tp * n_cfg - 1, give_flow, 0)
 
     pairs = rows // 2
     lane2 = lax.broadcasted_iota(jnp.int32, (pairs, HDIM), 1)
@@ -643,11 +646,11 @@
             device_id={"seq": seq_peer(k)}, device_id_type=MESH,
         )
 
-    def give_sum(k, carry):
-        sum_copy(k, me).start()
-        return carry
-
-    lax.fori_loop(1, n_seq, give_sum, 0)
+    def give_sum(t, carry):
+        sum_copy(far_first(t, n_seq), me).start()
+        return carry
+
+    lax.fori_loop(0, n_seq - 1, give_sum, 0)
 
     def take_sum(k, carry):
         sum_copy(k, seq_peer(k)).wait_recv()

time: 97.9 us -> 97.9 us (level)
  no operation moved by 1% of the time
where the time goes in v7:
time: 97.9 us; the launch traced here: 97.8 us
  Pallas kernels  95.3 us (97%)
  local copies, waits for them, and re-layouts  1.77 us (2%)
    pallas_call x1, Pallas kernels, local(): pl.pallas_call(functools.partial(kernel, rim), out_shape=(jax.ShapeDtypeS...  95.3 us

profile of v7, /device:TPU:1, one launch (start us, length us, event | category | flops | bytes accessed | tf_op | source)
XLA Modules:
  0.0 97.8 jit_solution(17793645764061467978)
XLA Ops:
  0.6 95.3 %flow_step.1 = (f32[64,192]{1,0:T(8,128)S(1)}, f32[64,192]{1,0:T(8,128)S(1)}, f32[1,3]{1,0:T(1,128)S(1)}) custom-call(s32[8]{0:T(128)} %counts_ref.1, s32[8]{0:T(128)} %widths_ref.1, s32[8]{0:T(128)} %steps_ref.1, f32[8]{0:T(128)} %guidance_ref.1, bf16[3,384,384]{2,1,0:T(8,128)(2,1)} %bitcast.13, bf16[384,3072]{1,0:T(8,128)(2,1)} %w_ref.1, ...), custom_call_target="tpu_custom_call" | custom-call | tf_op jit(solution)/shard_map/flow_step/pallas_call | solution.py:739
  96.0 0.6 copy.19
  96.6 0.6 copy.20
  97.2 0.5 copy.21
